TPU v7x, 128 devices: a whole 4x4x4 slice. The times are simulated.
128 devices in a mesh: tok: 16 (over x, y), head: 8 (over z, core).
Axes of the slice: x: 4, y: 4, z: 4, core: 2. Of those that a mesh axis runs over, the one named last changes fastest.
Arguments:
- hidden_in: bfloat16 [16384, 2048], P(('tok', 'head')), may hold values from -6 to 6
- attn_gain: float32 [2048], replicated, may hold values from 0.1 to 1.9
- w_qkv: bfloat16 [2048, 2560], P('tok'), may hold values from -0.125 to 0.125
- w_out: bfloat16 [2048, 2048], P('tok'), may hold values from -0.125 to 0.125
- mlp_gain: float32 [2048], replicated, may hold values from 0.1 to 1.9
- w_gate: bfloat16 [2048, 5632], P('tok', 'head'), may hold values from -0.125 to 0.125
- w_up: bfloat16 [2048, 5632], P('tok', 'head'), may hold values from -0.125 to 0.125
- w_down: bfloat16 [5632, 2048], P('head', 'tok'), may hold values from -0.078125 to 0.078125
- cache_kv: bfloat16 [32, 8, 4352, 128], P('tok', 'head'), may hold values from -240 to 240
- cached_len: int32 [32], P('tok'), may hold values from 0 to 8192, as said below
Outputs:
- hidden_out: bfloat16 [16384, 2048], P(('tok', 'head'))
- cache_out: bfloat16 [32, 8, 4352, 128], P('tok', 'head')
Inputs may be any that keep to these rules, and one draw needn't show every extreme that they name: `cached_len`: some request has exactly 8192 cached positions.
All inputs are finite; a program needn't handle non-finite values.
Results may differ from a plain program's by a relative error of at most 0.014.
Values may be sent and summed in bfloat16 or wider, within the bound.
No kernel may reach another device: no remote copies, remote signals or barrier semaphores. Data moves between devices by JAX's collectives and lax.ppermute only.
A program may use at most 128 MiB of HBM per device.

v0:
```python
import jax
import jax.numpy as jnp
from jax import lax
from jax.experimental import pallas as pl
from jax.experimental.pallas import tpu as pltpu
from jax.sharding import PartitionSpec as P

HEADS = 32
KV_HEADS = 4
HEAD_DIM = 64
S_NEW = 512
ROPE_BASE = 10000.0

KEYS = 512
ALIGN = 16
WINDOW = S_NEW + ALIGN
LOG2_E = 1.4426950408889634
VROWS = HEAD_DIM + 16


Z = 4
FF_PAIR = 128


def mean_norm(values, gain):
    widened = values.astype(jnp.float32)
    spread = jnp.mean(widened * widened, axis=-1, keepdims=True)
    return (widened * lax.rsqrt(spread + 1e-05) * gain).astype(jnp.bfloat16)


def contract(left_rows, right_rows):
    return jnp.dot(left_rows, right_rows, preferred_element_type=jnp.float32)


def in_hbm(array):
    return pltpu.with_memory_space_constraint(array, pltpu.HBM)


def exchange(array):
    return lax.ppermute(array, "head", [(i, i ^ 1) for i in range(lax.axis_size("head"))])


def along_z(array, distance):
    count = lax.axis_size("head")
    return lax.ppermute(array, "head", [(i, (i + 2 * distance) % count) for i in range(count)])


def gather_head(array):
    same_core = jnp.stack([array] + [along_z(array, d) for d in range(1, Z)])
    return same_core, exchange(same_core)


def sources():
    head_index = lax.axis_index("head")
    z, core = head_index // 2, head_index % 2
    chips = (z - jnp.arange(Z)) % Z * 2
    return jnp.concatenate([chips + core, chips + 1 - core]).astype(jnp.int32)


def attend(length, kv_ref, qt_ref, acc_ref, top_ref, out_ref):
    lanes = kv_ref.shape[1]
    acc_ref[...] = jnp.zeros(acc_ref.shape, jnp.float32)
    top_ref[...] = jnp.full(top_ref.shape, -1e30, jnp.float32)

    def step(index, masked, here):
        at = pl.multiple_of(index * KEYS, KEYS)
        block = kv_ref[pl.ds(at, KEYS)].astype(jnp.float32)
        on_key = lax.broadcasted_iota(jnp.int32, (KEYS, lanes), 1) < HEAD_DIM
        values = jnp.where(on_key, 1.0, block).T[HEAD_DIM - 16 :].astype(jnp.bfloat16)
        keys = jnp.where(on_key, block, pltpu.roll(block, HEAD_DIM, 1)).astype(jnp.bfloat16)
        scores = contract(keys, qt_ref[:, here])
        if masked:
            key = lax.broadcasted_iota(jnp.int32, scores.shape, 0) + (index * KEYS - length)
            query = lax.broadcasted_iota(jnp.int32, scores.shape, 1)
            scores = jnp.where(key <= query, scores, -jnp.inf)
        old_top = top_ref[:, here]
        top = jnp.maximum(jnp.max(scores, axis=0, keepdims=True), old_top)
        exps = jnp.exp2(scores - top).astype(jnp.bfloat16)
        acc_ref[:, here] = contract(values, exps) + acc_ref[:, here] * jnp.exp2(old_top - top)
        top_ref[:, here] = top

    def last(index, carry):
        def one_head(h, inner):
            step(index, True, pl.ds(pl.multiple_of(h * S_NEW, S_NEW), S_NEW))
            return inner

        return lax.fori_loop(0, qt_ref.shape[1] // S_NEW, one_head, carry)

    def full(index, carry):
        step(index, False, slice(None))
        return carry

    tail = length // KEYS
    lax.fori_loop(tail, (length + S_NEW + KEYS - 1) // KEYS, last, 0)
    lax.fori_loop(0, tail, full, 0)
    for pair in range(qt_ref.shape[1] // (2 * S_NEW)):
        sides = []
        for h in (2 * pair, 2 * pair + 1):
            here = slice(h * S_NEW, (h + 1) * S_NEW)
            sides.append(acc_ref[16:, here] / acc_ref[:1, here])
        out_ref[:, pair * lanes : (pair + 1) * lanes] = (
            jnp.concatenate(sides, axis=0).T.astype(jnp.bfloat16)
        )


def prepare_kernel(
    lens_ref, part_ref, src_ref, gain_ref, cos_ref, sin_ref, w_ref, x_0, x_1, x_2, x_3, x_others,
    own_hbm, other_hbm, qt_0, qt_1, kv_0, kv_1, cache_hbm, rows_hbm, x_ref, kv_ref, new_ref,
    qt_ref, x_sems, load_sems, store_sems,
):
    req_count, block_pos, lanes = own_hbm.shape
    heads_dev = qt_0.shape[1] // S_NEW
    half = HEAD_DIM // 2
    x_pieces = [x_0, x_1, x_2, x_3] + [x_others.at[i] for i in range(Z)]
    piece_rows = x_0.shape[0]
    own_at = pl.multiple_of(part_ref[0] * block_pos, ALIGN)
    other_at = pl.multiple_of((1 - part_ref[0]) * block_pos, ALIGN)

    def x_load(i):
        at = pl.multiple_of(src_ref[i] * piece_rows, piece_rows)
        return pltpu.make_async_copy(x_pieces[i], x_ref.at[pl.ds(at, piece_rows)], x_sems.at[i])

    def loads(r):
        return (
            pltpu.make_async_copy(
                own_hbm.at[r], kv_ref.at[r, pl.ds(own_at, block_pos)], load_sems.at[r, 0]
            ),
            pltpu.make_async_copy(
                other_hbm.at[r], kv_ref.at[r, pl.ds(other_at, block_pos)], load_sems.at[r, 1]
            ),
        )

    def stores(r):
        return (
            pltpu.make_async_copy(
                kv_ref.at[r, pl.ds(own_at, block_pos)], cache_hbm.at[r], store_sems.at[r, 0]
            ),
            pltpu.make_async_copy(kv_ref.at[r], (kv_0, kv_1)[r], store_sems.at[r, 1]),
            pltpu.make_async_copy(qt_ref.at[r], (qt_0, qt_1)[r], store_sems.at[r, 2]),
        )

    for i in range(2 * Z):
        x_load(i).start()
    for r in range(req_count):
        for copy in loads(r):
            copy.start()
    for i in range(2 * Z):
        x_load(i).wait()
    keep = pltpu.make_async_copy(x_ref, rows_hbm, store_sems.at[req_count, 0])
    keep.start()

    q_lanes = heads_dev * HEAD_DIM
    gain = gain_ref[...]
    def project(r, carry):
        here = pl.ds(pl.multiple_of(r * S_NEW, S_NEW), S_NEW)
        cosine = cos_ref[:, here]
        sine = sin_ref[:, here]

        def turn(block, scale):
            first = block[:half]
            second = block[half:]
            return jnp.concatenate(
                [
                    (first * cosine - second * sine) * scale,
                    (second * cosine + first * sine) * scale,
                ],
                axis=0,
            )

        normed = mean_norm(x_ref[here], gain)
        projected = contract(normed, w_ref[...])
        for pair in range(heads_dev // 2):
            flipped = projected[:, pair * lanes : (pair + 1) * lanes].T
            for one in range(2):
                rows = turn(flipped[one * HEAD_DIM : (one + 1) * HEAD_DIM], HEAD_DIM**-0.5)
                rows = rows.astype(jnp.bfloat16).astype(jnp.float32) * LOG2_E
                upper = rows.astype(jnp.bfloat16)
                lower = (rows - upper.astype(jnp.float32)).astype(jnp.bfloat16)
                at = (2 * pair + one) * S_NEW
                qt_ref[r, :HEAD_DIM, at : at + S_NEW] = upper
                qt_ref[r, HEAD_DIM:, at : at + S_NEW] = lower
        flipped = projected[:, q_lanes:].T
        fresh = jnp.concatenate([turn(flipped[:HEAD_DIM], 1.0), flipped[HEAD_DIM:]], axis=0)
        new_ref[r] = fresh.T.astype(jnp.bfloat16)
        return carry

    lax.fori_loop(0, req_count, project, 0)

    for r in range(req_count):
        length = lens_ref[r]
        for copy in loads(r):
            copy.wait()
        shift = length % ALIGN
        window_at = pl.multiple_of(length - shift, ALIGN)
        row = lax.broadcasted_iota(jnp.int32, (WINDOW, S_NEW), 0)
        col = lax.broadcasted_iota(jnp.int32, (WINDOW, S_NEW), 1)
        pick = (row - shift == col).astype(jnp.float32).astype(jnp.bfloat16)
        moved = contract(pick, new_ref[r])
        row = lax.broadcasted_iota(jnp.int32, (WINDOW, lanes), 0)
        inside = (row >= shift) & (row < shift + S_NEW)
        old = kv_ref[r, pl.ds(window_at, WINDOW)].astype(jnp.float32)
        kv_ref[r, pl.ds(window_at, WINDOW)] = jnp.where(inside, moved, old).astype(jnp.bfloat16)
        for copy in stores(r):
            copy.start()

    for r in range(req_count):
        for copy in stores(r):
            copy.wait()
    keep.wait()


def prepare(lens, part, src, gain, cosine, sine, w, x_same, x_others, own, other):
    req_count, block_pos, lanes = own.shape
    piece_rows, width = x_same[0].shape
    rows = piece_rows * 2 * Z
    heads_dev = (w.shape[1] - lanes) // HEAD_DIM
    positions = 2 * block_pos + ALIGN
    whole = pl.BlockSpec(memory_space=pltpu.VMEM)
    scalar = pl.BlockSpec(memory_space=pltpu.SMEM)
    remote = pl.BlockSpec(memory_space=pl.ANY)
    return pl.pallas_call(
        prepare_kernel,
        out_shape=(
            pltpu.HBM((lanes, heads_dev * S_NEW), jnp.bfloat16),
            pltpu.HBM((lanes, heads_dev * S_NEW), jnp.bfloat16),
            pltpu.HBM((positions, lanes), jnp.bfloat16),
            pltpu.HBM((positions, lanes), jnp.bfloat16),
            pltpu.HBM(own.shape, jnp.bfloat16),
            pltpu.HBM((rows, width), jnp.bfloat16),
        ),
        in_specs=[scalar] * 3 + [whole] * 4 + [remote] * (Z + 3),
        out_specs=(pl.BlockSpec(memory_space=pltpu.HBM),) * 6,
        scratch_shapes=[
            pltpu.VMEM((rows, width), jnp.bfloat16),
            pltpu.VMEM((req_count, positions, lanes), jnp.bfloat16),
            pltpu.VMEM((req_count, S_NEW, lanes), jnp.bfloat16),
            pltpu.VMEM((req_count, lanes, heads_dev * S_NEW), jnp.bfloat16),
            pltpu.SemaphoreType.DMA((2 * Z,)),
            pltpu.SemaphoreType.DMA((req_count, 2)),
            pltpu.SemaphoreType.DMA((req_count + 1, 3)),
        ],
        compiler_params=pltpu.CompilerParams(vmem_limit_bytes=22 << 20),
        cost_estimate=pl.CostEstimate(
            flops=4 * 10**9, transcendentals=10**6, bytes_accessed=20 * 10**6
        ),
        name="prepare",
    )(lens, part, src, gain, cosine, sine, w, *x_same, x_others, in_hbm(own), other)


def attention_kernel(len_ref, qt_hbm, kv_hbm, out_ref, qt_ref, kv_ref, acc_ref, top_ref, sems):
    loads = (
        pltpu.make_async_copy(qt_hbm, qt_ref, sems.at[0]),
        pltpu.make_async_copy(kv_hbm, kv_ref, sems.at[1]),
    )
    for copy in loads:
        copy.start()
    for copy in loads:
        copy.wait()
    attend(len_ref[0], kv_ref, qt_ref, acc_ref, top_ref, out_ref)


def attention(length, qt, kv):
    columns = qt.shape[1]
    remote = pl.BlockSpec(memory_space=pltpu.HBM)
    return pl.pallas_call(
        attention_kernel,
        out_shape=jax.ShapeDtypeStruct((S_NEW, columns // S_NEW * HEAD_DIM), jnp.bfloat16),
        in_specs=[pl.BlockSpec(memory_space=pltpu.SMEM), remote, remote],
        out_specs=pl.BlockSpec(memory_space=pltpu.VMEM),
        scratch_shapes=[
            pltpu.VMEM(qt.shape, jnp.bfloat16),
            pltpu.VMEM(kv.shape, jnp.bfloat16),
            pltpu.VMEM((VROWS, columns), jnp.float32),
            pltpu.VMEM((1, columns), jnp.float32),
            pltpu.SemaphoreType.DMA((2,)),
        ],
        compiler_params=pltpu.CompilerParams(vmem_limit_bytes=16 << 20),
        cost_estimate=pl.CostEstimate(
            flops=4 * 10**10, transcendentals=10**8, bytes_accessed=100 * 10**6
        ),
        name="attention",
    )(length, in_hbm(qt), in_hbm(kv))


def out_kernel(
    src_ref, request_ref, gain_ref, rows_hbm, w_same, w_others, a_same, a_others, residual_hbm,
    normed_hbm, att_ref, w_ref, sum_ref, rows_ref, normed_ref, row_sem, out_sems, w_sems,
):
    def w_load(side, i):
        source = (w_same, w_others)[side]
        return pltpu.make_async_copy(source.at[i], w_ref.at[side, i], w_sems.at[side, i])

    full_rows = rows_ref.shape[0]
    at = pl.multiple_of(request_ref[0] * full_rows, full_rows)
    load = pltpu.make_async_copy(rows_hbm.at[pl.ds(at, full_rows)], rows_ref, row_sem)
    for i in range(Z):
        w_load(0, i).start()
        w_load(1, i).start()
    load.start()
    for i in range(Z):
        att_ref[src_ref[i]] = a_same[i]
        att_ref[src_ref[Z + i]] = a_others[i]

    def columns(i, carry):
        attended = jnp.concatenate([att_ref[j] for j in range(2 * Z)], axis=1)
        w_load(0, i).wait()
        w_load(1, i).wait()
        sum_ref[src_ref[i]] = contract(attended, w_ref[0, i])
        sum_ref[src_ref[Z + i]] = contract(attended, w_ref[1, i])
        return carry

    lax.fori_loop(0, Z, columns, 0)
    load.wait()
    total = jnp.concatenate([sum_ref[i] for i in range(2 * Z)], axis=1)
    rows_ref[...] = (rows_ref[...].astype(jnp.float32) + total).astype(jnp.bfloat16)
    keep = pltpu.make_async_copy(rows_ref, residual_hbm, out_sems.at[0])
    keep.start()
    normed_ref[...] = mean_norm(rows_ref[...], gain_ref[...])
    give = pltpu.make_async_copy(normed_ref, normed_hbm, out_sems.at[1])
    give.start()
    keep.wait()
    give.wait()


def project_out(src, gain, weights, rows, pieces, request):
    piece_rows, piece_width = pieces[0].shape[1:]
    width = rows.shape[1]
    cols = weights[0].shape[2]
    scalar = pl.BlockSpec(memory_space=pltpu.SMEM)
    whole = pl.BlockSpec(memory_space=pltpu.VMEM)
    remote = pl.BlockSpec(memory_space=pltpu.HBM)
    return pl.pallas_call(
        out_kernel,
        out_shape=(pltpu.HBM((piece_rows, width), jnp.bfloat16),) * 2,
        in_specs=[scalar, scalar, whole] + [remote] * 3 + [whole] * 2,
        out_specs=(pl.BlockSpec(memory_space=pltpu.HBM),) * 2,
        scratch_shapes=[
            pltpu.VMEM((2 * Z, piece_rows, piece_width), jnp.bfloat16),
            pltpu.VMEM((2, Z, width, cols), jnp.bfloat16),
            pltpu.VMEM((2 * Z, piece_rows, cols), jnp.float32),
            pltpu.VMEM((piece_rows, width), jnp.bfloat16),
            pltpu.VMEM((piece_rows, width), jnp.bfloat16),
            pltpu.SemaphoreType.DMA,
            pltpu.SemaphoreType.DMA((2,)),
            pltpu.SemaphoreType.DMA((2, Z)),
        ],
        compiler_params=pltpu.CompilerParams(vmem_limit_bytes=27 << 20),
        cost_estimate=pl.CostEstimate(
            flops=4 * 10**9, transcendentals=0, bytes_accessed=16 * 10**6
        ),
        name="project_out",
    )(src, jnp.full((1,), request, jnp.int32), gain, in_hbm(rows), *map(in_hbm, weights), *pieces)


def ff_kernel(
    place_ref, low_hbm, high_hbm, w_ref, mine_ref, theirs_ref, x_ref, hidden_ref, x_sems
):
    shards, height, lanes = w_ref.shape
    width = x_ref.shape[3]
    units = hidden_ref.shape[1]
    rows = x_ref.shape[2]
    count = low_hbm.shape[0]
    row_at = pl.multiple_of(place_ref[1] * rows, rows)
    x_loads = []
    for i in range(2 * count):
        side = lax.rem(place_ref[0] + i % 2, 2)
        x_loads.append(
            pltpu.make_async_copy(
                (low_hbm, high_hbm)[i // count].at[i % count, pl.ds(row_at, rows)],
                x_ref.at[side, i // 2],
                x_sems.at[i],
            )
        )
    for copy in x_loads:
        copy.start()
    for copy in x_loads:
        copy.wait()
    x = x_ref[...].reshape(2 * Z * rows, width)
    for i in range(0, units, FF_PAIR):
        size = min(FF_PAIR, units - i)
        both = lax.dot_general(
            x,
            jnp.concatenate(
                [
                    jnp.concatenate([w_ref[j, at : at + size] for j in range(shards)], axis=1)
                    for at in (i, units + i)
                ],
                axis=0,
            ),
            (((1,), (1,)), ((), ())),
            preferred_element_type=jnp.float32,
        )
        hidden_ref[:, i : i + size] = (jax.nn.silu(both[:, :size]) * both[:, size:]).astype(
            jnp.bfloat16
        )
    hidden = hidden_ref[...]
    for i in range(0, shards, 2):
        down = jnp.concatenate([w_ref[i, 2 * units :], w_ref[i + 1, 2 * units :]], axis=1)
        terms = contract(hidden, down).astype(jnp.bfloat16).reshape(2, Z, rows, 2 * lanes)
        mine_ref[:, :, i * lanes : (i + 2) * lanes] = terms[0]
        theirs_ref[:, :, i * lanes : (i + 2) * lanes] = terms[1]


def feed_forward(place, low, high, weights, units):
    count, group_rows, width = low.shape
    rows = group_rows // 2
    whole = pl.BlockSpec(memory_space=pltpu.VMEM)
    remote = pl.BlockSpec(memory_space=pl.ANY)
    return pl.pallas_call(
        ff_kernel,
        out_shape=(jax.ShapeDtypeStruct((Z, rows, width), jnp.bfloat16),) * 2,
        in_specs=[pl.BlockSpec(memory_space=pltpu.SMEM), remote, remote, whole],
        out_specs=(whole, whole),
        scratch_shapes=[
            pltpu.VMEM((2, Z, rows, width), jnp.bfloat16),
            pltpu.VMEM((2 * count * rows, units), jnp.bfloat16),
            pltpu.SemaphoreType.DMA((2 * count,)),
        ],
        compiler_params=pltpu.CompilerParams(vmem_limit_bytes=12 << 20),
        cost_estimate=pl.CostEstimate(
            flops=5 * 10**9, transcendentals=10**6, bytes_accessed=16 * 10**6
        ),
        name="feed_forward",
    )(place, in_hbm(low), in_hbm(high), weights)


def angles_of(cached_len):
    half = HEAD_DIM // 2
    frequency = ROPE_BASE ** (-jnp.arange(half).astype(jnp.float32) * 2.0 / HEAD_DIM)
    positions = (cached_len[:, None] + jnp.arange(S_NEW)[None, :]).reshape(-1)
    angles = frequency[:, None] * positions.astype(jnp.float32)[None, :]
    return jnp.cos(angles), jnp.sin(angles)


def per_device(
    hidden_in, attn_gain, w_qkv, w_out, mlp_gain, w_gate, w_up, w_down, cache_kv, cached_len
):
    head_count = lax.axis_size("head")
    head_index = lax.axis_index("head")
    q_width = HEADS * HEAD_DIM
    kv_width = KV_HEADS * HEAD_DIM
    q_dev = q_width // head_count
    split_count = head_count // KV_HEADS
    part_index = head_index % split_count
    kv_head = head_index // split_count
    units = w_gate.shape[1]
    half_z = Z // 2
    row_count, width = hidden_in.shape

    src = sources()
    own = cache_kv[:, 0]
    other = exchange(own)
    columns = jnp.concatenate(
        [
            lax.dynamic_slice_in_dim(w_qkv, head_index * q_dev, q_dev, 1),
            lax.dynamic_slice_in_dim(w_qkv, q_width + kv_head * HEAD_DIM, HEAD_DIM, 1),
            lax.dynamic_slice_in_dim(w_qkv, q_width + kv_width + kv_head * HEAD_DIM, HEAD_DIM, 1),
        ],
        axis=1,
    )
    spread = jnp.broadcast_to(columns[None], (lax.axis_size("tok"), *columns.shape))
    spread, x_own = lax.optimization_barrier((spread, hidden_in))
    group_w = lax.all_to_all(spread, "tok", 0, 0, tiled=True).reshape(width, columns.shape[1])
    x_same = [x_own] + [along_z(x_own, d) for d in range(1, Z)]
    out_cols = width // head_count
    out_pair = lax.all_gather(
        jnp.concatenate(
            [
                lax.dynamic_slice_in_dim(w_out, block * out_cols, out_cols, 1)
                for block in (head_index, (head_index + half_z * 2) % head_count)
            ],
            axis=1,
        ),
        "tok", axis=0, tiled=True,
    )
    x_others = exchange(jnp.stack(x_same))
    ff_part, group_w, other, *_ = lax.optimization_barrier(
        (jnp.concatenate([w_gate.T, w_up.T, w_down], axis=0), group_w, other, *x_same)
    )
    ff_weights = lax.all_gather(ff_part, "tok", axis=0)
    cosine, sine = angles_of(cached_len)
    qt_0, qt_1, kv_0, kv_1, cache_new, rows = prepare(
        cached_len, part_index.reshape(1), src, attn_gain[None], cosine, sine, group_w,
        x_same, x_others, own, other,
    )
    out_pair, qt_0 = lax.optimization_barrier((out_pair, qt_0))
    att_0 = attention(cached_len[:1], qt_0, kv_0)
    out_part = out_pair[:, :out_cols]
    out_far = [along_z(out_part, 1), along_z(out_part, Z - 1)]
    att_0, out_part, out_pair, *out_far = lax.optimization_barrier(
        (att_0, out_part, out_pair, *out_far)
    )
    out_same = jnp.stack([out_part, out_far[0], out_pair[:, out_cols:], out_far[1]])
    out_pieces = (out_same, exchange(out_same))
    far_0 = [along_z(att_0, d) for d in range(1, Z)]
    att_1 = attention(cached_len[1:], qt_1, kv_1)
    att_1, att_0, *far_0 = lax.optimization_barrier((att_1, att_0, *far_0))
    same_0 = jnp.stack([att_0] + far_0)
    pieces_0 = (same_0, exchange(same_0))
    far_1 = [along_z(att_1, d) for d in range(1, Z)]
    gain = mlp_gain[None]
    residual_0, normed_0 = project_out(src, gain, out_pieces, rows, pieces_0, 0)
    att_1, residual_0, ff_weights, *far_1 = lax.optimization_barrier(
        (att_1, residual_0, ff_weights, *far_1)
    )
    same_1 = jnp.stack([att_1] + far_1)
    pieces_1 = (same_1, exchange(same_1))
    residual_1, normed_1 = project_out(src, gain, out_pieces, rows, pieces_1, 1)
    half_count = head_count // 2
    low = normed_0.reshape(half_count, row_count, width)
    high = normed_1.reshape(half_count, row_count, width)
    z = head_index // 2
    core = head_index % 2
    own_0 = lax.dynamic_index_in_dim(
        residual_0.reshape(half_count, row_count, width), head_index % half_count, 0, keepdims=False
    )
    own_1 = lax.dynamic_index_in_dim(
        residual_1.reshape(half_count, row_count, width), head_index % half_count, 0, keepdims=False
    )
    residual = jnp.where(head_index < half_count, own_0, own_1)
    outs = []
    for chunk in range(2):
        place = jnp.stack([core, jnp.int32(chunk)]).astype(jnp.int32)
        mine, theirs = feed_forward(place, low, high, ff_weights, units)
        pair = (mine.astype(jnp.float32) + exchange(theirs).astype(jnp.float32)).astype(
            jnp.bfloat16
        )
        rows_here = row_count // 2
        total = residual[chunk * rows_here : (chunk + 1) * rows_here].astype(jnp.float32)
        total = total + lax.dynamic_index_in_dim(pair, z, 0, keepdims=False).astype(jnp.float32)
        for d in range(1, Z):
            sent = lax.dynamic_index_in_dim(pair, (z + d) % Z, 0, keepdims=False)
            total = total + along_z(sent, d).astype(jnp.float32)
        outs.append(total.astype(jnp.bfloat16))
    return (jnp.concatenate(outs), cache_new[:, None])


def solution(mesh):
    return jax.shard_map(
        per_device,
        mesh=mesh,
        in_specs=(
            P(("tok", "head"), None),
            P(),
            P("tok", None),
            P("tok", None),
            P(),
            P("tok", "head"),
            P("tok", "head"),
            P("head", "tok"),
            P("tok", "head", None, None),
            P("tok"),
        ),
        out_specs=(P(("tok", "head"), None), P("tok", "head", None, None)),
        check_vma=False,
    )
```

profile of v0, /device:TPU:0, one launch (start us, length us, event | category | flops | bytes accessed | tf_op | source)
XLA Modules:
  0.0 216.7 jit_solution(13383349289846395288)
XLA Ops:
  12.1 7.1 %all-to-all-start = ((bf16[16,128,384]{2,1,0:T(8,128)(2,1)}), bf16[16,128,384]{2,1,0:T(8,128)(2,1)S(1)}, u32[]{:S(2)}, u32[]{:S(2)}) async-start(bf16[16,128,384]{2,1,0:T(8,128)(2,1)} %broadcast_in_dim.9), calls=%async_computation | async-start | bytes 3145728 | tf_op jit(solution)/shard_map/all_to_all | solution.py:463
  19.3 2.0 collective-permute-start.1
  21.3 3.6 %collective-permute-start.2 = (bf16[128,2048]{1,0:T(8,128)(2,1)S(1)}, bf16[128,2048]{1,0:T(8,128)(2,1)S(1)}, u32[]{:S(2)}, u32[]{:S(2)}) collective-permute-start(bf16[128,2048]{1,0:T(8,128)(2,1)S(1)} %copy-done), channel_id=1, source_target_pairs={{0,4},{1,5},{2,6},{3,7},{4,0},{5,1},{6,2},{7,3},{8,12},{9,13},{10,... | collective-permute-start | bytes 1572872 | tf_op jit(solution)/shard_map/ppermute | solution.py:45
  25.9 1.8 pad_maximum_fusion.4
  27.6 8.0 %collective-permute-done.1.x_1 = bf16[128,2048]{1,0:T(8,128)(2,1)S(1)} collective-permute-done((bf16[128,2048]{1,0:T(8,128)(2,1)S(1)}, bf16[128,2048]{1,0:T(8,128)(2,1)S(1)}, u32[]{:S(2)}, u32[]{:S(2)}) %collective-permute-start.1) | collective-permute-done | bytes 524320 | tf_op jit(solution)/shard_map/ppermute | solution.py:45
  35.7 12.4 %collective-permute-done.2.x_2 = bf16[128,2048]{1,0:T(8,128)(2,1)S(1)} collective-permute-done((bf16[128,2048]{1,0:T(8,128)(2,1)S(1)}, bf16[128,2048]{1,0:T(8,128)(2,1)S(1)}, u32[]{:S(2)}, u32[]{:S(2)}) %collective-permute-start.2) | collective-permute-done | bytes 524320 | tf_op jit(solution)/shard_map/ppermute | solution.py:45
  48.2 2.6 %pad_maximum_fusion.1 = bf16[4,128,2048]{2,1,0:T(8,128)(2,1)} fusion(bf16[1,128,2048]{2,1,0:T(8,128)(2,1)} %bitcast.9, bf16[1,128,2048]{2,1,0:T(8,128)(2,1)S(1)} %bitcast.66, bf16[1,128,2048]{2,1,0:T(8,128)(2,1)S(1)} %bitcast.65, bf16[1,128,2048]{2,1,0:T(8,128)(2,1)S(1)} %bitcast.64), kind=kLoop, calls=%fused_computation.1 | loop fusion | flops 3145728 | bytes 4194304 | tf_op jit(solution)/shard_map/stack | solution.py:476
  52.1 3.2 %collective-permute-done.4.x_others = bf16[4,128,2048]{2,1,0:T(8,128)(2,1)} collective-permute-done((bf16[4,128,2048]{2,1,0:T(8,128)(2,1)}, bf16[4,128,2048]{2,1,0:T(8,128)(2,1)}, u32[]{:S(2)}, u32[]{:S(2)}) %collective-permute-start.4) | collective-permute-done | bytes 2097184 | tf_op jit(solution)/shard_map/ppermute | solution.py:40
  55.3 10.9 %prepare.1 = (bf16[128,2048]{1,0:T(8,128)(2,1)}, bf16[128,2048]{1,0:T(8,128)(2,1)}, bf16[8720,128]{1,0:T(8,128)(2,1)}, bf16[8720,128]{1,0:T(8,128)(2,1)}, bf16[2...) custom-call(s32[2]{0:T(128)S(1)} %copy-done.1, s32[1]{0:T(128)} %bitcast.part_ref, s32[8]{0:T(128)S(1)} %pad_add_fusion.src_ref, ...), custom_call_target="tpu_custom_call" | custom-call | flops 4000000000 | bytes 20000000 | tf_op jit(solution)/shard_map/prepare/pallas_call | solution.py:221
  66.2 3.2 %all-gather.4.cloned.1.call-done = bf16[2048,512]{1,0:T(8,128)(2,1)} async-done(((bf16[128,512]{1,0:T(8,128)(2,1)}), bf16[2048,512]{1,0:T(8,128)(2,1)}) %all-gather.4.cloned.1.call-update) | async-done | bytes 2097168 | tf_op jit(solution)/shard_map/all_gather | solution.py:466
  70.7 1.6 collective-permute-start.5
  72.3 1.7 collective-permute-start.6
  74.0 12.8 %attention.3 = bf16[512,256]{1,0:T(8,128)(2,1)S(1)} custom-call(s32[1]{0:T(128)} %get-tuple-element.93.len_ref, bf16[128,2048]{1,0:T(8,128)(2,1)} %get-tuple-element.46.qt_hbm, bf16[8720,128]{1,0:T(8,128)(2,1)} %get-tuple-element.47.kv_hbm), custom_call_target="tpu_custom_call" | custom-call | flops 40000000000 | bytes 100000000 | tf_op jit(solution)/shard_map/attention/pallas_call | solution.py:265
  86.7 9.3 %collective-permute-done.5 = bf16[2048,256]{1,0:T(8,128)(2,1)S(1)} collective-permute-done((bf16[2048,256]{1,0:T(8,128)(2,1)S(1)}, bf16[2048,256]{1,0:T(8,128)(2,1)S(1)}, u32[]{:S(2)}, u32[]{:S(2)}) %collective-permute-start.5) | collective-permute-done | bytes 1048608 | tf_op jit(solution)/shard_map/ppermute | solution.py:45
  96.1 1.6 collective-permute-start.7
  97.6 2.9 %collective-permute-start.8 = (bf16[512,256]{1,0:T(8,128)(2,1)S(1)}, bf16[512,256]{1,0:T(8,128)(2,1)S(1)}, u32[]{:S(2)}, u32[]{:S(2)}) collective-permute-start(bf16[512,256]{1,0:T(8,128)(2,1)S(1)} %attention.3), channel_id=1, source_target_pairs={{0,4},{1,5},{2,6},{3,7},{4,0},{5,1},{6,2},{7,3},{8,12},{9,13},{10,... | collective-permute-start | bytes 786440 | tf_op jit(solution)/shard_map/ppermute | solution.py:45
  102.3 29.8 %attention.2 = bf16[512,256]{1,0:T(8,128)(2,1)S(1)} custom-call(s32[1]{0:T(128)} %get-tuple-element.92.len_ref, bf16[128,2048]{1,0:T(8,128)(2,1)} %get-tuple-element.43.qt_hbm, bf16[8720,128]{1,0:T(8,128)(2,1)} %get-tuple-element.44.kv_hbm), custom_call_target="tpu_custom_call" | custom-call | flops 40000000000 | bytes 100000000 | tf_op jit(solution)/shard_map/attention/pallas_call | solution.py:265
  133.6 2.2 %collective-permute-start.14 = (bf16[512,256]{1,0:T(8,128)(2,1)S(1)}, bf16[512,256]{1,0:T(8,128)(2,1)S(1)}, u32[]{:S(2)}, u32[]{:S(2)}) collective-permute-start(bf16[512,256]{1,0:T(8,128)(2,1)S(1)} %attention.2), channel_id=1, source_target_pairs={{0,6},{1,7},{2,0},{3,1},{4,2},{5,3},{6,4},{7,5},{8,14},{9,15},{10,... | collective-permute-start | bytes 786440 | tf_op jit(solution)/shard_map/ppermute | solution.py:45
  135.9 2.0 copy-done.10
  137.8 10.5 %project_out.2 = (bf16[512,2048]{1,0:T(8,128)(2,1)}, bf16[512,2048]{1,0:T(8,128)(2,1)}) custom-call(s32[8]{0:T(128)S(1)} %pad_add_fusion.src_ref, s32[1]{0:T(128)} %constant.136.clone.1.request_ref, f32[1,2048]{1,0:T(1,128)S(1)} %bitcast.72, bf16[1024,2048]{1,0:T(8,128)(2,1)} %get-tuple-element.51.rows_hbm, bf16[4,2048,256]{2,1,0:T(8,128)(2,1)} %copy-done.6, ...), custom_call_target="tpu_custom_call" | custom-call | flops 4000000000 | bytes 16000000 | tf_op jit(solution)/shard_map/project_out/pallas_call | solution.py:332
  148.9 2.6 %collective-permute-done.15.a_others = bf16[4,512,256]{2,1,0:T(8,128)(2,1)S(1)} collective-permute-done((bf16[4,512,256]{2,1,0:T(8,128)(2,1)S(1)}, bf16[4,512,256]{2,1,0:T(8,128)(2,1)S(1)}, u32[]{:S(2)}, u32[]{:S(2)}) %collective-permute-start.15) | collective-permute-done | bytes 1048608 | tf_op jit(solution)/shard_map/ppermute | solution.py:40
  151.5 10.6 %project_out.3 = (bf16[512,2048]{1,0:T(8,128)(2,1)}, bf16[512,2048]{1,0:T(8,128)(2,1)}) custom-call(s32[8]{0:T(128)S(1)} %pad_add_fusion.src_ref, s32[1]{0:T(128)} %constant.137.clone.1.request_ref, f32[1,2048]{1,0:T(1,128)S(1)} %bitcast.73, bf16[1024,2048]{1,0:T(8,128)(2,1)} %get-tuple-element.51.rows_hbm, bf16[4,2048,256]{2,1,0:T(8,128)(2,1)} %copy-done.6, ...), custom_call_target="tpu_custom_call" | custom-call | flops 4000000000 | bytes 16000000 | tf_op jit(solution)/shard_map/project_out/pallas_call | solution.py:332
  162.1 8.2 %feed_forward.3 = (bf16[4,64,2048]{2,1,0:T(8,128)(2,1)S(1)}, bf16[4,64,2048]{2,1,0:T(8,128)(2,1)}) custom-call(s32[2]{0:T(128)S(1)} %get-tuple-element.95.place_ref, bf16[4,128,2048]{2,1,0:T(8,128)(2,1)} %bitcast.91, bf16[4,128,2048]{2,1,0:T(8,128)(2,1)} %bitcast.93, bf16[16,2112,128]{2,1,0:T(8,128)(2,1)S(1)} %bitcast.69), custom_call_target="tpu_custom_call" | custom-call | flops 5000000000 | bytes 16000000 | tf_op jit(solution)/shard_map/feed_forward/pallas_call | solution.py:409
  170.8 7.2 %feed_forward.2 = (bf16[4,64,2048]{2,1,0:T(8,128)(2,1)S(1)}, bf16[4,64,2048]{2,1,0:T(8,128)(2,1)S(1)}) custom-call(s32[2]{0:T(128)S(1)} %get-tuple-element.94.place_ref, bf16[4,128,2048]{2,1,0:T(8,128)(2,1)} %bitcast.92, bf16[4,128,2048]{2,1,0:T(8,128)(2,1)} %bitcast.94, bf16[16,2112,128]{2,1,0:T(8,128)(2,1)S(1)} %bitcast.70), custom_call_target="tpu_custom_call" | custom-call | flops 5000000000 | bytes 16000000 | tf_op jit(solution)/shard_map/feed_forward/pallas_call | solution.py:409
  178.5 1.6 add_convert_fusion
  180.9 3.2 %collective-permute-start.22 = (bf16[64,2048]{1,0:T(8,128)(2,1)S(1)}, bf16[64,2048]{1,0:T(8,128)(2,1)S(1)}, u32[]{:S(2)}, u32[]{:S(2)}) collective-permute-start(bf16[64,2048]{1,0:T(8,128)(2,1)S(1)} %get-tuple-element.83), channel_id=1, source_target_pairs={{0,4},{1,5},{2,6},{3,7},{4,0},{5,1},{6,2},{7,3},{8,12},{9,13},{10,... | collective-permute-start | bytes 786440 | tf_op jit(solution)/shard_map/ppermute | solution.py:45
  185.5 1.6 add_convert_fusion.1
  190.1 1.7 collective-permute-start.19
  193.0 3.8 %collective-permute-done.22 = bf16[64,2048]{1,0:T(8,128)(2,1)S(1)} collective-permute-done((bf16[64,2048]{1,0:T(8,128)(2,1)S(1)}, bf16[64,2048]{1,0:T(8,128)(2,1)S(1)}, u32[]{:S(2)}, u32[]{:S(2)}) %collective-permute-start.22) | collective-permute-done | bytes 262176 | tf_op jit(solution)/shard_map/ppermute | solution.py:45
  197.2 4.4 %collective-permute-done.17 = bf16[64,2048]{1,0:T(8,128)(2,1)S(1)} collective-permute-done((bf16[64,2048]{1,0:T(8,128)(2,1)S(1)}, bf16[64,2048]{1,0:T(8,128)(2,1)S(1)}, u32[]{:S(2)}, u32[]{:S(2)}) %collective-permute-start.17) | collective-permute-done | bytes 262176 | tf_op jit(solution)/shard_map/ppermute | solution.py:45
  201.6 5.8 %collective-permute-done.18 = bf16[64,2048]{1,0:T(8,128)(2,1)} collective-permute-done((bf16[64,2048]{1,0:T(8,128)(2,1)S(1)}, bf16[64,2048]{1,0:T(8,128)(2,1)}, u32[]{:S(2)}, u32[]{:S(2)}) %collective-permute-start.18) | collective-permute-done | bytes 262176 | tf_op jit(solution)/shard_map/ppermute | solution.py:45
  207.5 1.5 fusion.5
  (81 shorter events, 20.8 us)
Async XLA Ops:
  7.2 62.2 %all-gather.4.cloned.1.call-start = ((), (), s32[]{:S(2)}) async-start(), calls=%async_computation.1 | async-start | bytes 2228224 | tf_op jit(solution)/shard_map/all_gather | solution.py:466
  8.8 39.3 %collective-permute-start = (bf16[2,4352,128]{2,1,0:T(8,128)(2,1)}, bf16[2,4352,128]{2,1,0:T(8,128)(2,1)}, u32[]{:S(2)}, u32[]{:S(2)}) collective-permute-start(bf16[2,4352,128]{2,1,0:T(8,128)(2,1)} %bitcast.88), channel_id=1, source_target_pairs={{0,1},{1,0},{2,3},{3,2},{4,5},{5,4},{6,7},{7,6},{8,9},{9,8},{10,11... | collective-permute-start | bytes 6684680 | tf_op jit(solution)/shard_map/ppermute | solution.py:40
  10.7 15.1 %copy-start.8 = (bf16[704,128]{1,0:T(8,128)(2,1)S(1)}, bf16[704,128]{1,0:T(8,128)(2,1)}, u32[]{:S(2)}) copy-start(bf16[704,128]{1,0:T(8,128)(2,1)} %param.17) | copy-start | bytes 540676
  10.8 15.1 %copy-start.9 = (bf16[128,704]{0,1:T(8,128)(2,1)S(1)}, bf16[128,704]{0,1:T(8,128)(2,1)}, u32[]{:S(2)}) copy-start(bf16[128,704]{0,1:T(8,128)(2,1)} %param.16) | copy-start | bytes 540676
  12.1 36.0 %all-to-all-start = ((bf16[16,128,384]{2,1,0:T(8,128)(2,1)}), bf16[16,128,384]{2,1,0:T(8,128)(2,1)S(1)}, u32[]{:S(2)}, u32[]{:S(2)}) async-start(bf16[16,128,384]{2,1,0:T(8,128)(2,1)} %broadcast_in_dim.9), calls=%async_computation | async-start | bytes 3145728 | tf_op jit(solution)/shard_map/all_to_all | solution.py:463
  19.2 129.4 %all-gather.6.cloned.1.call-start = ((), (), s32[]{:S(2)}) async-start(), calls=%async_computation.2 | async-start | bytes 9191424 | tf_op jit(solution)/shard_map/all_gather | solution.py:480
  19.3 16.4 %collective-permute-start.1 = (bf16[128,2048]{1,0:T(8,128)(2,1)S(1)}, bf16[128,2048]{1,0:T(8,128)(2,1)S(1)}, u32[]{:S(2)}, u32[]{:S(2)}) collective-permute-start(bf16[128,2048]{1,0:T(8,128)(2,1)S(1)} %copy-done), channel_id=1, source_target_pairs={{0,2},{1,3},{2,4},{3,5},{4,6},{5,7},{6,0},{7,1},{8,10},{9,11},{10,... | collective-permute-start | bytes 1572872 | tf_op jit(solution)/shard_map/ppermute | solution.py:45
  21.3 26.8 %collective-permute-start.2 = (bf16[128,2048]{1,0:T(8,128)(2,1)S(1)}, bf16[128,2048]{1,0:T(8,128)(2,1)S(1)}, u32[]{:S(2)}, u32[]{:S(2)}) collective-permute-start(bf16[128,2048]{1,0:T(8,128)(2,1)S(1)} %copy-done), channel_id=1, source_target_pairs={{0,4},{1,5},{2,6},{3,7},{4,0},{5,1},{6,2},{7,3},{8,12},{9,13},{10,... | collective-permute-start | bytes 1572872 | tf_op jit(solution)/shard_map/ppermute | solution.py:45
  24.9 23.2 %collective-permute-start.3 = (bf16[128,2048]{1,0:T(8,128)(2,1)S(1)}, bf16[128,2048]{1,0:T(8,128)(2,1)}, u32[]{:S(2)}, u32[]{:S(2)}) collective-permute-start(bf16[128,2048]{1,0:T(8,128)(2,1)S(1)} %copy-done), channel_id=1, source_target_pairs={{0,6},{1,7},{2,0},{3,1},{4,2},{5,3},{6,4},{7,5},{8,14},{9,15},{10,... | collective-permute-start | bytes 1572872 | tf_op jit(solution)/shard_map/ppermute | solution.py:45
  50.8 4.5 %collective-permute-start.4 = (bf16[4,128,2048]{2,1,0:T(8,128)(2,1)}, bf16[4,128,2048]{2,1,0:T(8,128)(2,1)}, u32[]{:S(2)}, u32[]{:S(2)}) collective-permute-start(bf16[4,128,2048]{2,1,0:T(8,128)(2,1)} %pad_maximum_fusion.1), channel_id=1, source_target_pairs={{0,1},{1,0},{2,3},{3,2},{4,5},{5,4},{6,7},{7,6},{8,9},{9,8},{10,11... | collective-permute-start | bytes 6291464 | tf_op jit(solution)/shard_map/ppermute | solution.py:40
  70.7 25.4 %collective-permute-start.5 = (bf16[2048,256]{1,0:T(8,128)(2,1)S(1)}, bf16[2048,256]{1,0:T(8,128)(2,1)S(1)}, u32[]{:S(2)}, u32[]{:S(2)}) collective-permute-start(bf16[2048,256]{1,0:T(8,128)(2,1)S(1)} %slice.22), channel_id=1, source_target_pairs={{0,2},{1,3},{2,4},{3,5},{4,6},{5,7},{6,0},{7,1},{8,10},{9,11},{10,... | collective-permute-start | bytes 3145736 | tf_op jit(solution)/shard_map/ppermute | solution.py:45
  72.3 23.8 %collective-permute-start.6 = (bf16[2048,256]{1,0:T(8,128)(2,1)S(1)}, bf16[2048,256]{1,0:T(8,128)(2,1)S(1)}, u32[]{:S(2)}, u32[]{:S(2)}) collective-permute-start(bf16[2048,256]{1,0:T(8,128)(2,1)S(1)} %slice.22), channel_id=1, source_target_pairs={{0,6},{1,7},{2,0},{3,1},{4,2},{5,3},{6,4},{7,5},{8,14},{9,15},{10,... | collective-permute-start | bytes 3145736 | tf_op jit(solution)/shard_map/ppermute | solution.py:45
  74.0 27.6 %copy-start.7 = (bf16[2048,512]{1,0:T(8,128)(2,1)S(1)}, bf16[2048,512]{1,0:T(8,128)(2,1)}, u32[]{:S(2)}) copy-start(bf16[2048,512]{1,0:T(8,128)(2,1)} %all-gather.4.cloned.1.call-done) | copy-start | bytes 6291460
  96.1 36.1 %collective-permute-start.7 = (bf16[512,256]{1,0:T(8,128)(2,1)S(1)}, bf16[512,256]{1,0:T(8,128)(2,1)S(1)}, u32[]{:S(2)}, u32[]{:S(2)}) collective-permute-start(bf16[512,256]{1,0:T(8,128)(2,1)S(1)} %attention.3), channel_id=1, source_target_pairs={{0,2},{1,3},{2,4},{3,5},{4,6},{5,7},{6,0},{7,1},{8,10},{9,11},{10,... | collective-permute-start | bytes 786440 | tf_op jit(solution)/shard_map/ppermute | solution.py:45
  97.6 34.6 %collective-permute-start.8 = (bf16[512,256]{1,0:T(8,128)(2,1)S(1)}, bf16[512,256]{1,0:T(8,128)(2,1)S(1)}, u32[]{:S(2)}, u32[]{:S(2)}) collective-permute-start(bf16[512,256]{1,0:T(8,128)(2,1)S(1)} %attention.3), channel_id=1, source_target_pairs={{0,4},{1,5},{2,6},{3,7},{4,0},{5,1},{6,2},{7,3},{8,12},{9,13},{10,... | collective-permute-start | bytes 786440 | tf_op jit(solution)/shard_map/ppermute | solution.py:45
  100.5 31.7 %collective-permute-start.9 = (bf16[512,256]{1,0:T(8,128)(2,1)S(1)}, bf16[512,256]{1,0:T(8,128)(2,1)S(1)}, u32[]{:S(2)}, u32[]{:S(2)}) collective-permute-start(bf16[512,256]{1,0:T(8,128)(2,1)S(1)} %attention.3), channel_id=1, source_target_pairs={{0,6},{1,7},{2,0},{3,1},{4,2},{5,3},{6,4},{7,5},{8,14},{9,15},{10,... | collective-permute-start | bytes 786440 | tf_op jit(solution)/shard_map/ppermute | solution.py:45
  102.2 29.9 %copy-start.6 = (bf16[4,2048,256]{2,1,0:T(8,128)(2,1)}, bf16[4,2048,256]{2,1,0:T(8,128)(2,1)S(1)}, u32[]{:S(2)}) copy-start(bf16[4,2048,256]{2,1,0:T(8,128)(2,1)S(1)} %pad_maximum_fusion.w_same) | copy-start | bytes 12582916
  102.2 33.6 %collective-permute-start.10 = (bf16[4,2048,256]{2,1,0:T(8,128)(2,1)S(1)}, bf16[4,2048,256]{2,1,0:T(8,128)(2,1)S(1)}, u32[]{:S(2)}, u32[]{:S(2)}) collective-permute-start(bf16[4,2048,256]{2,1,0:T(8,128)(2,1)S(1)} %pad_maximum_fusion.w_same), channel_id=1, source_target_pairs={{0,1},{1,0},{2,3},{3,2},{4,5},{5,4},{6,7},{7,6},{8,9},{9,8},{10,11... | collective-permute-start | bytes 12582920 | tf_op jit(solution)/shard_map/ppermute | solution.py:40
  132.4 3.5 %collective-permute-start.11 = (bf16[4,512,256]{2,1,0:T(8,128)(2,1)S(1)}, bf16[4,512,256]{2,1,0:T(8,128)(2,1)S(1)}, u32[]{:S(2)}, u32[]{:S(2)}) collective-permute-start(bf16[4,512,256]{2,1,0:T(8,128)(2,1)S(1)} %pad_maximum_fusion.2.a_same), channel_id=1, source_target_pairs={{0,1},{1,0},{2,3},{3,2},{4,5},{5,4},{6,7},{7,6},{8,9},{9,8},{10,11... | collective-permute-start | bytes 3145736 | tf_op jit(solution)/shard_map/ppermute | solution.py:40
  132.5 15.9 %collective-permute-start.12 = (bf16[512,256]{1,0:T(8,128)(2,1)S(1)}, bf16[512,256]{1,0:T(8,128)(2,1)S(1)}, u32[]{:S(2)}, u32[]{:S(2)}) collective-permute-start(bf16[512,256]{1,0:T(8,128)(2,1)S(1)} %attention.2), channel_id=1, source_target_pairs={{0,2},{1,3},{2,4},{3,5},{4,6},{5,7},{6,0},{7,1},{8,10},{9,11},{10,... | collective-permute-start | bytes 786440 | tf_op jit(solution)/shard_map/ppermute | solution.py:45
  133.1 15.3 %collective-permute-start.13 = (bf16[512,256]{1,0:T(8,128)(2,1)S(1)}, bf16[512,256]{1,0:T(8,128)(2,1)S(1)}, u32[]{:S(2)}, u32[]{:S(2)}) collective-permute-start(bf16[512,256]{1,0:T(8,128)(2,1)S(1)} %attention.2), channel_id=1, source_target_pairs={{0,4},{1,5},{2,6},{3,7},{4,0},{5,1},{6,2},{7,3},{8,12},{9,13},{10,... | collective-permute-start | bytes 786440 | tf_op jit(solution)/shard_map/ppermute | solution.py:45
  133.6 15.0 %collective-permute-start.14 = (bf16[512,256]{1,0:T(8,128)(2,1)S(1)}, bf16[512,256]{1,0:T(8,128)(2,1)S(1)}, u32[]{:S(2)}, u32[]{:S(2)}) collective-permute-start(bf16[512,256]{1,0:T(8,128)(2,1)S(1)} %attention.2), channel_id=1, source_target_pairs={{0,6},{1,7},{2,0},{3,1},{4,2},{5,3},{6,4},{7,5},{8,14},{9,15},{10,... | collective-permute-start | bytes 786440 | tf_op jit(solution)/shard_map/ppermute | solution.py:45
  148.8 2.7 %collective-permute-start.15 = (bf16[4,512,256]{2,1,0:T(8,128)(2,1)S(1)}, bf16[4,512,256]{2,1,0:T(8,128)(2,1)S(1)}, u32[]{:S(2)}, u32[]{:S(2)}) collective-permute-start(bf16[4,512,256]{2,1,0:T(8,128)(2,1)S(1)} %pad_maximum_fusion.3.a_same), channel_id=1, source_target_pairs={{0,1},{1,0},{2,3},{3,2},{4,5},{5,4},{6,7},{7,6},{8,9},{9,8},{10,11... | collective-permute-start | bytes 3145736 | tf_op jit(solution)/shard_map/ppermute | solution.py:40
  148.9 13.2 %copy-start.2 = (bf16[33792,128]{1,0:T(8,128)(2,1)S(1)}, bf16[33792,128]{1,0:T(8,128)(2,1)}, u32[]{:S(2)}) copy-start(bf16[33792,128]{1,0:T(8,128)(2,1)} %all-gather.6.cloned.1.call-done) | copy-start | bytes 25952260
  170.4 8.1 %collective-permute-start.20 = (bf16[4,64,2048]{2,1,0:T(8,128)(2,1)}, bf16[4,64,2048]{2,1,0:T(8,128)(2,1)}, u32[]{:S(2)}, u32[]{:S(2)}) collective-permute-start(bf16[4,64,2048]{2,1,0:T(8,128)(2,1)} %get-tuple-element.74), channel_id=1, source_target_pairs={{0,1},{1,0},{2,3},{3,2},{4,5},{5,4},{6,7},{7,6},{8,9},{9,8},{10,11... | collective-permute-start | bytes 3145736 | tf_op jit(solution)/shard_map/ppermute | solution.py:40
  178.0 7.5 %collective-permute-start.16 = (bf16[4,64,2048]{2,1,0:T(8,128)(2,1)S(1)}, bf16[4,64,2048]{2,1,0:T(8,128)(2,1)}, u32[]{:S(2)}, u32[]{:S(2)}) collective-permute-start(bf16[4,64,2048]{2,1,0:T(8,128)(2,1)S(1)} %get-tuple-element.72), channel_id=1, source_target_pairs={{0,1},{1,0},{2,3},{3,2},{4,5},{5,4},{6,7},{7,6},{8,9},{9,8},{10,11... | collective-permute-start | bytes 3145736 | tf_op jit(solution)/shard_map/ppermute | solution.py:40
  180.2 9.9 %collective-permute-start.21 = (bf16[64,2048]{1,0:T(8,128)(2,1)S(1)}, bf16[64,2048]{1,0:T(8,128)(2,1)S(1)}, u32[]{:S(2)}, u32[]{:S(2)}) collective-permute-start(bf16[64,2048]{1,0:T(8,128)(2,1)S(1)} %get-tuple-element.81), channel_id=1, source_target_pairs={{0,2},{1,3},{2,4},{3,5},{4,6},{5,7},{6,0},{7,1},{8,10},{9,11},{10,... | collective-permute-start | bytes 786440 | tf_op jit(solution)/shard_map/ppermute | solution.py:45
  180.9 16.0 %collective-permute-start.22 = (bf16[64,2048]{1,0:T(8,128)(2,1)S(1)}, bf16[64,2048]{1,0:T(8,128)(2,1)S(1)}, u32[]{:S(2)}, u32[]{:S(2)}) collective-permute-start(bf16[64,2048]{1,0:T(8,128)(2,1)S(1)} %get-tuple-element.83), channel_id=1, source_target_pairs={{0,4},{1,5},{2,6},{3,7},{4,0},{5,1},{6,2},{7,3},{8,12},{9,13},{10,... | collective-permute-start | bytes 786440 | tf_op jit(solution)/shard_map/ppermute | solution.py:45
  184.1 13.1 %collective-permute-start.23 = (bf16[64,2048]{1,0:T(8,128)(2,1)S(1)}, bf16[64,2048]{1,0:T(8,128)(2,1)S(1)}, u32[]{:S(2)}, u32[]{:S(2)}) collective-permute-start(bf16[64,2048]{1,0:T(8,128)(2,1)S(1)} %get-tuple-element.82), channel_id=1, source_target_pairs={{0,6},{1,7},{2,0},{3,1},{4,2},{5,3},{6,4},{7,5},{8,14},{9,15},{10,... | collective-permute-start | bytes 786440 | tf_op jit(solution)/shard_map/ppermute | solution.py:45
  187.3 14.4 %collective-permute-start.17 = (bf16[64,2048]{1,0:T(8,128)(2,1)S(1)}, bf16[64,2048]{1,0:T(8,128)(2,1)S(1)}, u32[]{:S(2)}, u32[]{:S(2)}) collective-permute-start(bf16[64,2048]{1,0:T(8,128)(2,1)S(1)} %get-tuple-element.78), channel_id=1, source_target_pairs={{0,2},{1,3},{2,4},{3,5},{4,6},{5,7},{6,0},{7,1},{8,10},{9,11},{10,... | collective-permute-start | bytes 786440 | tf_op jit(solution)/shard_map/ppermute | solution.py:45
  187.9 19.5 %collective-permute-start.18 = (bf16[64,2048]{1,0:T(8,128)(2,1)S(1)}, bf16[64,2048]{1,0:T(8,128)(2,1)}, u32[]{:S(2)}, u32[]{:S(2)}) collective-permute-start(bf16[64,2048]{1,0:T(8,128)(2,1)S(1)} %get-tuple-element.80), channel_id=1, source_target_pairs={{0,4},{1,5},{2,6},{3,7},{4,0},{5,1},{6,2},{7,3},{8,12},{9,13},{10,... | collective-permute-start | bytes 786440 | tf_op jit(solution)/shard_map/ppermute | solution.py:45
  190.1 17.4 %collective-permute-start.19 = (bf16[64,2048]{1,0:T(8,128)(2,1)S(1)}, bf16[64,2048]{1,0:T(8,128)(2,1)}, u32[]{:S(2)}, u32[]{:S(2)}) collective-permute-start(bf16[64,2048]{1,0:T(8,128)(2,1)S(1)} %get-tuple-element.79), channel_id=1, source_target_pairs={{0,6},{1,7},{2,0},{3,1},{4,2},{5,3},{6,4},{7,5},{8,14},{9,15},{10,... | collective-permute-start | bytes 786440 | tf_op jit(solution)/shard_map/ppermute | solution.py:45
  (6 other events, 33.1 us)
Sparse Core Ops, SparseCore 0:
  10.1 59.1 all-gather.3
  71.5 71.2 all-gather.5
where the time goes:
time: 219 us; the launch traced here: 217 us
  Pallas kernels  90.1 us (41%)
  waiting for transfers between devices  54.7 us (25%)
  starting transfers between devices  35.8 us (16%)
  between operations  14.4 us (7%)
  other arithmetic  13.6 us (6%)
  local copies, waits for them, and re-layouts  8.12 us (4%)
    ppermute x17, waiting for transfers between devices, along_z(): lax.ppermute(array, 'head', [(i, (i + 2 * distance) % count) for i in ran...  45.8 us
    pallas_call x2, Pallas kernels, attention(): pl.pallas_call(attention_kernel, out_shape=jax.ShapeDtypeStruct((S_NEW, c...  42.6 us
    ppermute x17, starting transfers between devices, along_z(): lax.ppermute(array, 'head', [(i, (i + 2 * distance) % count) for i in ran...  27.3 us
    pallas_call x2, Pallas kernels, project_out(): pl.pallas_call(out_kernel, out_shape=(pltpu.HBM((piece_rows, width), jnp....  21.1 us
    pallas_call x2, Pallas kernels, feed_forward(): pl.pallas_call(ff_kernel, out_shape=(jax.ShapeDtypeStruct((Z, rows, width...  15.4 us
    pallas_call x1, Pallas kernels, prepare(): pl.pallas_call(prepare_kernel, out_shape=(pltpu.HBM((lanes, heads_dev * S...  10.9 us
    all_to_all x1, starting transfers between devices, per_device(): lax.all_to_all(spread, 'tok', 0, 0, tiled=True)  7.12 us
    ppermute x7, waiting for transfers between devices, exchange(): lax.ppermute(array, 'head', [(i, i ^ 1) for i in range(lax.axis_size('hea...  5.75 us
  transfers between devices with their start and end apart: 27, of which 14 were waited for; matrix products, arithmetic and copies ran while one was open for 7% of the time, Pallas kernels for 33%

commit v1 on v0

--- a/solution.py
+++ b/solution.py
@@ -105,11 +105,10 @@
 
 def prepare_kernel(
     lens_ref, part_ref, src_ref, gain_ref, cos_ref, sin_ref, w_ref, x_0, x_1, x_2, x_3, x_others,
-    own_hbm, other_hbm, qt_0, qt_1, kv_0, kv_1, cache_hbm, rows_hbm, x_ref, kv_ref, new_ref,
-    qt_ref, x_sems, load_sems, store_sems,
+    own_hbm, other_hbm, qt_hbm, kv_hbm, cache_hbm, rows_hbm, x_ref, kv_ref, new_ref, qt_ref, x_sems, load_sems, store_sems,
 ):
     req_count, block_pos, lanes = own_hbm.shape
-    heads_dev = qt_0.shape[1] // S_NEW
+    heads_dev = qt_ref.shape[2] // S_NEW
     half = HEAD_DIM // 2
     x_pieces = [x_0, x_1, x_2, x_3] + [x_others.at[i] for i in range(Z)]
     piece_rows = x_0.shape[0]
@@ -135,8 +134,8 @@
             pltpu.make_async_copy(
                 kv_ref.at[r, pl.ds(own_at, block_pos)], cache_hbm.at[r], store_sems.at[r, 0]
             ),
-            pltpu.make_async_copy(kv_ref.at[r], (kv_0, kv_1)[r], store_sems.at[r, 1]),
-            pltpu.make_async_copy(qt_ref.at[r], (qt_0, qt_1)[r], store_sems.at[r, 2]),
+            pltpu.make_async_copy(kv_ref.at[r], kv_hbm.at[r], store_sems.at[r, 1]),
+            pltpu.make_async_copy(qt_ref.at[r], qt_hbm.at[r], store_sems.at[r, 2]),
         )
 
     for i in range(2 * Z):
@@ -182,11 +181,7 @@
         flipped = projected[:, q_lanes:].T
         fresh = jnp.concatenate([turn(flipped[:HEAD_DIM], 1.0), flipped[HEAD_DIM:]], axis=0)
         new_ref[r] = fresh.T.astype(jnp.bfloat16)
-        return carry
-
-    lax.fori_loop(0, req_count, project, 0)
-
-    for r in range(req_count):
+
         length = lens_ref[r]
         for copy in loads(r):
             copy.wait()
@@ -202,7 +197,9 @@
         kv_ref[r, pl.ds(window_at, WINDOW)] = jnp.where(inside, moved, old).astype(jnp.bfloat16)
         for copy in stores(r):
             copy.start()
-
+        return carry
+
+    lax.fori_loop(0, req_count, project, 0)
     for r in range(req_count):
         for copy in stores(r):
             copy.wait()
@@ -221,15 +218,13 @@
     return pl.pallas_call(
         prepare_kernel,
         out_shape=(
-            pltpu.HBM((lanes, heads_dev * S_NEW), jnp.bfloat16),
-            pltpu.HBM((lanes, heads_dev * S_NEW), jnp.bfloat16),
-            pltpu.HBM((positions, lanes), jnp.bfloat16),
-            pltpu.HBM((positions, lanes), jnp.bfloat16),
+            pltpu.HBM((req_count, lanes, heads_dev * S_NEW), jnp.bfloat16),
+            pltpu.HBM((req_count, positions, lanes), jnp.bfloat16),
             pltpu.HBM(own.shape, jnp.bfloat16),
             pltpu.HBM((rows, width), jnp.bfloat16),
         ),
         in_specs=[scalar] * 3 + [whole] * 4 + [remote] * (Z + 3),
-        out_specs=(pl.BlockSpec(memory_space=pltpu.HBM),) * 6,
+        out_specs=(pl.BlockSpec(memory_space=pltpu.HBM),) * 4,
         scratch_shapes=[
             pltpu.VMEM((rows, width), jnp.bfloat16),
             pltpu.VMEM((req_count, positions, lanes), jnp.bfloat16),
@@ -247,20 +242,20 @@
     )(lens, part, src, gain, cosine, sine, w, *x_same, x_others, in_hbm(own), other)
 
 
-def attention_kernel(len_ref, qt_hbm, kv_hbm, out_ref, qt_ref, kv_ref, acc_ref, top_ref, sems):
+def attention_kernel(which_ref, qt_hbm, kv_hbm, out_ref, qt_ref, kv_ref, acc_ref, top_ref, sems):
     loads = (
-        pltpu.make_async_copy(qt_hbm, qt_ref, sems.at[0]),
-        pltpu.make_async_copy(kv_hbm, kv_ref, sems.at[1]),
+        pltpu.make_async_copy(qt_hbm.at[which_ref[1]], qt_ref, sems.at[0]),
+        pltpu.make_async_copy(kv_hbm.at[which_ref[1]], kv_ref, sems.at[1]),
     )
     for copy in loads:
         copy.start()
     for copy in loads:
         copy.wait()
-    attend(len_ref[0], kv_ref, qt_ref, acc_ref, top_ref, out_ref)
-
-
-def attention(length, qt, kv):
-    columns = qt.shape[1]
+    attend(which_ref[0], kv_ref, qt_ref, acc_ref, top_ref, out_ref)
+
+
+def attention(lens, request, qt, kv):
+    columns = qt.shape[2]
     remote = pl.BlockSpec(memory_space=pltpu.HBM)
     return pl.pallas_call(
         attention_kernel,
@@ -268,8 +263,8 @@
         in_specs=[pl.BlockSpec(memory_space=pltpu.SMEM), remote, remote],
         out_specs=pl.BlockSpec(memory_space=pltpu.VMEM),
         scratch_shapes=[
-            pltpu.VMEM(qt.shape, jnp.bfloat16),
-            pltpu.VMEM(kv.shape, jnp.bfloat16),
+            pltpu.VMEM(qt.shape[1:], jnp.bfloat16),
+            pltpu.VMEM(kv.shape[1:], jnp.bfloat16),
             pltpu.VMEM((VROWS, columns), jnp.float32),
             pltpu.VMEM((1, columns), jnp.float32),
             pltpu.SemaphoreType.DMA((2,)),
@@ -279,23 +274,28 @@
             flops=4 * 10**10, transcendentals=10**8, bytes_accessed=100 * 10**6
         ),
         name="attention",
-    )(length, in_hbm(qt), in_hbm(kv))
+    )(jnp.stack([lens[request], jnp.int32(request)]), in_hbm(qt), in_hbm(kv))
 
 
 def out_kernel(
-    src_ref, request_ref, gain_ref, rows_hbm, w_same, w_others, a_same, a_others, residual_hbm,
-    normed_hbm, att_ref, w_ref, sum_ref, rows_ref, normed_ref, row_sem, out_sems, w_sems,
+    src_ref, request_ref, gain_ref, rows_hbm, pair_0, near_0, far_0, pair_1, near_1, far_1, a_same,
+    a_others, residual_hbm, normed_hbm, att_ref, w_ref, sum_ref, rows_ref, normed_ref, row_sem, out_sems, w_sems,
 ):
-    def w_load(side, i):
-        source = (w_same, w_others)[side]
-        return pltpu.make_async_copy(source.at[i], w_ref.at[side, i], w_sems.at[side, i])
+    cols = near_0.shape[1]
+    sources = [
+        (pair.at[:, pl.ds(0, cols)], near, pair.at[:, pl.ds(cols, cols)], far)
+        for pair, near, far in ((pair_0, near_0, far_0), (pair_1, near_1, far_1))
+    ]
+
+    def w_load(side, i, source=near_0):
+        return pltpu.make_async_copy(source, w_ref.at[side, i], w_sems.at[side, i])
 
     full_rows = rows_ref.shape[0]
     at = pl.multiple_of(request_ref[0] * full_rows, full_rows)
     load = pltpu.make_async_copy(rows_hbm.at[pl.ds(at, full_rows)], rows_ref, row_sem)
     for i in range(Z):
-        w_load(0, i).start()
-        w_load(1, i).start()
+        w_load(0, i, sources[0][i]).start()
+        w_load(1, i, sources[1][i]).start()
     load.start()
     for i in range(Z):
         att_ref[src_ref[i]] = a_same[i]
@@ -325,14 +325,14 @@
 def project_out(src, gain, weights, rows, pieces, request):
     piece_rows, piece_width = pieces[0].shape[1:]
     width = rows.shape[1]
-    cols = weights[0].shape[2]
+    cols = weights[1].shape[1]
     scalar = pl.BlockSpec(memory_space=pltpu.SMEM)
     whole = pl.BlockSpec(memory_space=pltpu.VMEM)
     remote = pl.BlockSpec(memory_space=pltpu.HBM)
     return pl.pallas_call(
         out_kernel,
         out_shape=(pltpu.HBM((piece_rows, width), jnp.bfloat16),) * 2,
-        in_specs=[scalar, scalar, whole] + [remote] * 3 + [whole] * 2,
+        in_specs=[scalar, scalar, whole] + [remote] * 7 + [whole] * 2,
         out_specs=(pl.BlockSpec(memory_space=pltpu.HBM),) * 2,
         scratch_shapes=[
             pltpu.VMEM((2 * Z, piece_rows, piece_width), jnp.bfloat16),
@@ -479,21 +479,19 @@
     )
     ff_weights = lax.all_gather(ff_part, "tok", axis=0)
     cosine, sine = angles_of(cached_len)
-    qt_0, qt_1, kv_0, kv_1, cache_new, rows = prepare(
+    qt, kv, cache_new, rows = prepare(
         cached_len, part_index.reshape(1), src, attn_gain[None], cosine, sine, group_w,
         x_same, x_others, own, other,
     )
-    out_pair, qt_0 = lax.optimization_barrier((out_pair, qt_0))
-    att_0 = attention(cached_len[:1], qt_0, kv_0)
+    out_pair, qt = lax.optimization_barrier((out_pair, qt))
+    att_0 = attention(cached_len, 0, qt, kv)
+    pair_other = exchange(out_pair)
     out_part = out_pair[:, :out_cols]
     out_far = [along_z(out_part, 1), along_z(out_part, Z - 1)]
-    att_0, out_part, out_pair, *out_far = lax.optimization_barrier(
-        (att_0, out_part, out_pair, *out_far)
-    )
-    out_same = jnp.stack([out_part, out_far[0], out_pair[:, out_cols:], out_far[1]])
-    out_pieces = (out_same, exchange(out_same))
+    att_0, qt, pair_other, *out_far = lax.optimization_barrier((att_0, qt, pair_other, *out_far))
+    out_pieces = (out_pair, *out_far, pair_other, *[exchange(piece) for piece in out_far])
     far_0 = [along_z(att_0, d) for d in range(1, Z)]
-    att_1 = attention(cached_len[1:], qt_1, kv_1)
+    att_1 = attention(cached_len, 1, qt, kv)
     att_1, att_0, *far_0 = lax.optimization_barrier((att_1, att_0, *far_0))
     same_0 = jnp.stack([att_0] + far_0)
     pieces_0 = (same_0, exchange(same_0))

time: 219 us -> 219 us (level)
  Pallas kernels: 90.1 us -> 99.8 us
  waiting for transfers between devices: 54.7 us -> 45.1 us
    pallas_call x2, Pallas kernels: 42.6 us -> 53.3 us  [attention(): pl.pallas_call(attention_kernel, out_shape=jax.ShapeDtypeStruct((S_NEW, c...]
    ppermute x17, waiting for transfers between devices: 45.8 us -> 36.4 us  [along_z(): lax.ppermute(array, 'head', [(i, (i + 2 * distance) % count) for i in ran...]
    ppermute x7 -> x9, waiting for transfers between devices: 5.75 us -> 4.26 us  [exchange(): lax.ppermute(array, 'head', [(i, i ^ 1) for i in range(lax.axis_size('hea...]
  transfers between devices with their start and end apart: 27 -> 29, of which waited for: 14 -> 11; matrix products, arithmetic and copies ran while one was open for 7% -> 8% of each run, Pallas kernels for 33% -> 37%
where the time goes in v1:
time: 219 us; the launch traced here: 217 us
  Pallas kernels  99.8 us (46%)
  waiting for transfers between devices  45.1 us (21%)
  starting transfers between devices  36.3 us (17%)
  other arithmetic  14.5 us (7%)
  between operations  14.5 us (7%)
  local copies, waits for them, and re-layouts  7.06 us (3%)
    pallas_call x2, Pallas kernels, attention(): pl.pallas_call(attention_kernel, out_shape=jax.ShapeDtypeStruct((S_NEW, c...  53.3 us
    ppermute x17, waiting for transfers between devices, along_z(): lax.ppermute(array, 'head', [(i, (i + 2 * distance) % count) for i in ran...  36.4 us
    ppermute x17, starting transfers between devices, along_z(): lax.ppermute(array, 'head', [(i, (i + 2 * distance) % count) for i in ran...  27.5 us
    pallas_call x2, Pallas kernels, project_out(): pl.pallas_call(out_kernel, out_shape=(pltpu.HBM((piece_rows, width), jnp....  21.2 us
    pallas_call x2, Pallas kernels, feed_forward(): pl.pallas_call(ff_kernel, out_shape=(jax.ShapeDtypeStruct((Z, rows, width...  15.4 us
    pallas_call x1, Pallas kernels, prepare(): pl.pallas_call(prepare_kernel, out_shape=(pltpu.HBM((req_count, lanes, he...  9.88 us
    all_to_all x1, starting transfers between devices, per_device(): lax.all_to_all(spread, 'tok', 0, 0, tiled=True)  7.12 us
  transfers between devices with their start and end apart: 29, of which 11 were waited for; matrix products, arithmetic and copies ran while one was open for 8% of the time, Pallas kernels for 37%

profile of v1, /device:TPU:0, one launch (start us, length us, event | category | flops | bytes accessed | tf_op | source)
XLA Modules:
  0.0 217.3 jit_solution(10310064545516551094)
XLA Ops:
  12.1 7.1 %all-to-all-start = ((bf16[16,128,384]{2,1,0:T(8,128)(2,1)}), bf16[16,128,384]{2,1,0:T(8,128)(2,1)S(1)}, u32[]{:S(2)}, u32[]{:S(2)}) async-start(bf16[16,128,384]{2,1,0:T(8,128)(2,1)} %broadcast_in_dim.9), calls=%async_computation | async-start | bytes 3145728 | tf_op jit(solution)/shard_map/all_to_all | solution.py:463
  19.3 2.0 collective-permute-start.1
  21.3 3.6 %collective-permute-start.2 = (bf16[128,2048]{1,0:T(8,128)(2,1)S(1)}, bf16[128,2048]{1,0:T(8,128)(2,1)S(1)}, u32[]{:S(2)}, u32[]{:S(2)}) collective-permute-start(bf16[128,2048]{1,0:T(8,128)(2,1)S(1)} %copy-done), channel_id=1, source_target_pairs={{0,4},{1,5},{2,6},{3,7},{4,0},{5,1},{6,2},{7,3},{8,12},{9,13},{10,... | collective-permute-start | bytes 1572872 | tf_op jit(solution)/shard_map/ppermute | solution.py:45
  25.9 1.8 pad_maximum_fusion.3
  27.7 8.0 %collective-permute-done.1.x_1 = bf16[128,2048]{1,0:T(8,128)(2,1)S(1)} collective-permute-done((bf16[128,2048]{1,0:T(8,128)(2,1)S(1)}, bf16[128,2048]{1,0:T(8,128)(2,1)S(1)}, u32[]{:S(2)}, u32[]{:S(2)}) %collective-permute-start.1) | collective-permute-done | bytes 524320 | tf_op jit(solution)/shard_map/ppermute | solution.py:45
  35.7 12.4 %collective-permute-done.2.x_2 = bf16[128,2048]{1,0:T(8,128)(2,1)S(1)} collective-permute-done((bf16[128,2048]{1,0:T(8,128)(2,1)S(1)}, bf16[128,2048]{1,0:T(8,128)(2,1)S(1)}, u32[]{:S(2)}, u32[]{:S(2)}) %collective-permute-start.2) | collective-permute-done | bytes 524320 | tf_op jit(solution)/shard_map/ppermute | solution.py:45
  48.2 2.6 %pad_maximum_fusion = bf16[4,128,2048]{2,1,0:T(8,128)(2,1)} fusion(bf16[1,128,2048]{2,1,0:T(8,128)(2,1)} %bitcast.9, bf16[1,128,2048]{2,1,0:T(8,128)(2,1)S(1)} %bitcast.61, bf16[1,128,2048]{2,1,0:T(8,128)(2,1)S(1)} %bitcast.60, bf16[1,128,2048]{2,1,0:T(8,128)(2,1)S(1)} %bitcast.59), kind=kLoop, calls=%fused_computation | loop fusion | flops 3145728 | bytes 4194304 | tf_op jit(solution)/shard_map/stack | solution.py:476
  53.6 1.7 collective-permute-done.4.x_others
  55.3 9.9 %prepare.1 = (bf16[2,128,2048]{2,1,0:T(8,128)(2,1)}, bf16[2,8720,128]{2,1,0:T(8,128)(2,1)}, bf16[2,4352,128]{2,1,0:T(8,128)(2,1)}, bf16[1024,2048]{1,0:T(8,128)(2,1)}) custom-call(s32[2]{0:T(128)S(1)} %copy-done.1, s32[1]{0:T(128)} %bitcast.part_ref, s32[8]{0:T(128)S(1)} %pad_add_fusion.4.src_ref, f32[1,2048]{1,0:T(1,128)S(1)} %bitcast.66, ...), custom_call_target="tpu_custom_call" | custom-call | flops 4000000000 | bytes 20000000 | tf_op jit(solution)/shard_map/prepare/pallas_call | solution.py:218
  65.2 4.4 %all-gather.4.cloned.1.call-done.pair_0 = bf16[2048,512]{1,0:T(8,128)(2,1)} async-done(((bf16[128,512]{1,0:T(8,128)(2,1)}), bf16[2048,512]{1,0:T(8,128)(2,1)}) %all-gather.4.cloned.1.call-update) | async-done | bytes 2097168 | tf_op jit(solution)/shard_map/all_gather | solution.py:466
  70.8 1.6 collective-permute-start.6
  72.5 1.7 collective-permute-start.7
  74.1 24.0 %attention.2 = bf16[512,256]{1,0:T(8,128)(2,1)S(1)} custom-call(s32[2]{0:T(128)S(1)} %pad_add_fusion.3.which_ref, bf16[2,128,2048]{2,1,0:T(8,128)(2,1)} %get-tuple-element.45.qt_hbm, bf16[2,8720,128]{2,1,0:T(8,128)(2,1)} %get-tuple-element.43.kv_hbm), custom_call_target="tpu_custom_call" | custom-call | flops 40000000000 | bytes 100000000 | tf_op jit(solution)/shard_map/attention/pallas_call | solution.py:260
  98.2 2.6 %collective-permute-start.10 = (bf16[512,256]{1,0:T(8,128)(2,1)S(1)}, bf16[512,256]{1,0:T(8,128)(2,1)S(1)}, u32[]{:S(2)}, u32[]{:S(2)}) collective-permute-start(bf16[512,256]{1,0:T(8,128)(2,1)S(1)} %attention.2), channel_id=1, source_target_pairs={{0,6},{1,7},{2,0},{3,1},{4,2},{5,3},{6,4},{7,5},{8,14},{9,15},{10,... | collective-permute-start | bytes 786440 | tf_op jit(solution)/shard_map/ppermute | solution.py:45
  100.8 1.9 collective-permute-start.9
  103.2 29.3 %attention.3 = bf16[512,256]{1,0:T(8,128)(2,1)S(1)} custom-call(s32[2]{0:T(128)S(1)} %pad_add_fusion.1.which_ref, bf16[2,128,2048]{2,1,0:T(8,128)(2,1)} %get-tuple-element.45.qt_hbm, bf16[2,8720,128]{2,1,0:T(8,128)(2,1)} %get-tuple-element.43.kv_hbm), custom_call_target="tpu_custom_call" | custom-call | flops 40000000000 | bytes 100000000 | tf_op jit(solution)/shard_map/attention/pallas_call | solution.py:260
  132.8 2.0 collective-permute-start.14
  135.0 2.6 %collective-permute-start.16 = (bf16[512,256]{1,0:T(8,128)(2,1)S(1)}, bf16[512,256]{1,0:T(8,128)(2,1)S(1)}, u32[]{:S(2)}, u32[]{:S(2)}) collective-permute-start(bf16[512,256]{1,0:T(8,128)(2,1)S(1)} %attention.3), channel_id=1, source_target_pairs={{0,6},{1,7},{2,0},{3,1},{4,2},{5,3},{6,4},{7,5},{8,14},{9,15},{10,... | collective-permute-start | bytes 786440 | tf_op jit(solution)/shard_map/ppermute | solution.py:45
  138.6 10.6 %project_out.2 = (bf16[512,2048]{1,0:T(8,128)(2,1)}, bf16[512,2048]{1,0:T(8,128)(2,1)}) custom-call(s32[8]{0:T(128)S(1)} %pad_add_fusion.4.src_ref, s32[1]{0:T(128)} %constant.121.clone.1.request_ref, f32[1,2048]{1,0:T(1,128)S(1)} %bitcast.67, bf16[1024,2048]{1,0:T(8,128)(2,1)} %get-tuple-element.48.rows_hbm, ...), custom_call_target="tpu_custom_call" | custom-call | flops 4000000000 | bytes 16000000 | tf_op jit(solution)/shard_map/project_out/pallas_call | solution.py:332
  149.6 2.6 %collective-permute-done.17.a_others = bf16[4,512,256]{2,1,0:T(8,128)(2,1)S(1)} collective-permute-done((bf16[4,512,256]{2,1,0:T(8,128)(2,1)S(1)}, bf16[4,512,256]{2,1,0:T(8,128)(2,1)S(1)}, u32[]{:S(2)}, u32[]{:S(2)}) %collective-permute-start.17) | collective-permute-done | bytes 1048608 | tf_op jit(solution)/shard_map/ppermute | solution.py:40
  152.2 10.6 %project_out.3 = (bf16[512,2048]{1,0:T(8,128)(2,1)}, bf16[512,2048]{1,0:T(8,128)(2,1)}) custom-call(s32[8]{0:T(128)S(1)} %pad_add_fusion.4.src_ref, s32[1]{0:T(128)} %constant.120.clone.1.request_ref, f32[1,2048]{1,0:T(1,128)S(1)} %bitcast.68, bf16[1024,2048]{1,0:T(8,128)(2,1)} %get-tuple-element.48.rows_hbm, ...), custom_call_target="tpu_custom_call" | custom-call | flops 4000000000 | bytes 16000000 | tf_op jit(solution)/shard_map/project_out/pallas_call | solution.py:332
  162.8 8.2 %feed_forward.3 = (bf16[4,64,2048]{2,1,0:T(8,128)(2,1)S(1)}, bf16[4,64,2048]{2,1,0:T(8,128)(2,1)}) custom-call(s32[2]{0:T(128)S(1)} %get-tuple-element.90.place_ref, bf16[4,128,2048]{2,1,0:T(8,128)(2,1)} %bitcast.83, bf16[4,128,2048]{2,1,0:T(8,128)(2,1)} %bitcast.85, bf16[16,2112,128]{2,1,0:T(8,128)(2,1)S(1)} %bitcast.64), custom_call_target="tpu_custom_call" | custom-call | flops 5000000000 | bytes 16000000 | tf_op jit(solution)/shard_map/feed_forward/pallas_call | solution.py:409
  171.4 7.2 %feed_forward.2 = (bf16[4,64,2048]{2,1,0:T(8,128)(2,1)S(1)}, bf16[4,64,2048]{2,1,0:T(8,128)(2,1)S(1)}) custom-call(s32[2]{0:T(128)S(1)} %get-tuple-element.91.place_ref, bf16[4,128,2048]{2,1,0:T(8,128)(2,1)} %bitcast.84, bf16[4,128,2048]{2,1,0:T(8,128)(2,1)} %bitcast.86, bf16[16,2112,128]{2,1,0:T(8,128)(2,1)S(1)} %bitcast.65), custom_call_target="tpu_custom_call" | custom-call | flops 5000000000 | bytes 16000000 | tf_op jit(solution)/shard_map/feed_forward/pallas_call | solution.py:409
  179.1 1.6 add_convert_fusion
  180.8 1.4 collective-permute-start.23
  182.2 2.5 %collective-permute-start.24 = (bf16[64,2048]{1,0:T(8,128)(2,1)S(1)}, bf16[64,2048]{1,0:T(8,128)(2,1)S(1)}, u32[]{:S(2)}, u32[]{:S(2)}) collective-permute-start(bf16[64,2048]{1,0:T(8,128)(2,1)S(1)} %get-tuple-element.79), channel_id=1, source_target_pairs={{0,4},{1,5},{2,6},{3,7},{4,0},{5,1},{6,2},{7,3},{8,12},{9,13},{10,... | collective-permute-start | bytes 786440 | tf_op jit(solution)/shard_map/ppermute | solution.py:45
  185.5 1.6 add_convert_fusion.1
  189.5 1.5 collective-permute-done.23
  193.6 3.8 %collective-permute-done.24 = bf16[64,2048]{1,0:T(8,128)(2,1)S(1)} collective-permute-done((bf16[64,2048]{1,0:T(8,128)(2,1)S(1)}, bf16[64,2048]{1,0:T(8,128)(2,1)S(1)}, u32[]{:S(2)}, u32[]{:S(2)}) %collective-permute-start.24) | collective-permute-done | bytes 262176 | tf_op jit(solution)/shard_map/ppermute | solution.py:45
  197.8 4.1 %collective-permute-done.19 = bf16[64,2048]{1,0:T(8,128)(2,1)S(1)} collective-permute-done((bf16[64,2048]{1,0:T(8,128)(2,1)S(1)}, bf16[64,2048]{1,0:T(8,128)(2,1)S(1)}, u32[]{:S(2)}, u32[]{:S(2)}) %collective-permute-start.19) | collective-permute-done | bytes 262176 | tf_op jit(solution)/shard_map/ppermute | solution.py:45
  202.0 6.0 %collective-permute-done.20 = bf16[64,2048]{1,0:T(8,128)(2,1)} collective-permute-done((bf16[64,2048]{1,0:T(8,128)(2,1)S(1)}, bf16[64,2048]{1,0:T(8,128)(2,1)}, u32[]{:S(2)}, u32[]{:S(2)}) %collective-permute-start.20) | collective-permute-done | bytes 262176 | tf_op jit(solution)/shard_map/ppermute | solution.py:45
  208.1 1.5 fusion.5
  (89 shorter events, 20.3 us)
Async XLA Ops:
  7.2 62.4 %all-gather.4.cloned.1.call-start = ((), (), s32[]{:S(2)}) async-start(), calls=%async_computation.1 | async-start | bytes 2228224 | tf_op jit(solution)/shard_map/all_gather | solution.py:466
  8.8 39.3 %collective-permute-start = (bf16[2,4352,128]{2,1,0:T(8,128)(2,1)}, bf16[2,4352,128]{2,1,0:T(8,128)(2,1)}, u32[]{:S(2)}, u32[]{:S(2)}) collective-permute-start(bf16[2,4352,128]{2,1,0:T(8,128)(2,1)} %bitcast.80), channel_id=1, source_target_pairs={{0,1},{1,0},{2,3},{3,2},{4,5},{5,4},{6,7},{7,6},{8,9},{9,8},{10,11... | collective-permute-start | bytes 6684680 | tf_op jit(solution)/shard_map/ppermute | solution.py:40
  12.1 36.0 %all-to-all-start = ((bf16[16,128,384]{2,1,0:T(8,128)(2,1)}), bf16[16,128,384]{2,1,0:T(8,128)(2,1)S(1)}, u32[]{:S(2)}, u32[]{:S(2)}) async-start(bf16[16,128,384]{2,1,0:T(8,128)(2,1)} %broadcast_in_dim.9), calls=%async_computation | async-start | bytes 3145728 | tf_op jit(solution)/shard_map/all_to_all | solution.py:463
  19.2 130.1 %all-gather.6.cloned.1.call-start = ((), (), s32[]{:S(2)}) async-start(), calls=%async_computation.2 | async-start | bytes 9191424 | tf_op jit(solution)/shard_map/all_gather | solution.py:480
  19.3 16.4 %collective-permute-start.1 = (bf16[128,2048]{1,0:T(8,128)(2,1)S(1)}, bf16[128,2048]{1,0:T(8,128)(2,1)S(1)}, u32[]{:S(2)}, u32[]{:S(2)}) collective-permute-start(bf16[128,2048]{1,0:T(8,128)(2,1)S(1)} %copy-done), channel_id=1, source_target_pairs={{0,2},{1,3},{2,4},{3,5},{4,6},{5,7},{6,0},{7,1},{8,10},{9,11},{10,... | collective-permute-start | bytes 1572872 | tf_op jit(solution)/shard_map/ppermute | solution.py:45
  21.3 26.8 %collective-permute-start.2 = (bf16[128,2048]{1,0:T(8,128)(2,1)S(1)}, bf16[128,2048]{1,0:T(8,128)(2,1)S(1)}, u32[]{:S(2)}, u32[]{:S(2)}) collective-permute-start(bf16[128,2048]{1,0:T(8,128)(2,1)S(1)} %copy-done), channel_id=1, source_target_pairs={{0,4},{1,5},{2,6},{3,7},{4,0},{5,1},{6,2},{7,3},{8,12},{9,13},{10,... | collective-permute-start | bytes 1572872 | tf_op jit(solution)/shard_map/ppermute | solution.py:45
  24.9 23.2 %collective-permute-start.3 = (bf16[128,2048]{1,0:T(8,128)(2,1)S(1)}, bf16[128,2048]{1,0:T(8,128)(2,1)}, u32[]{:S(2)}, u32[]{:S(2)}) collective-permute-start(bf16[128,2048]{1,0:T(8,128)(2,1)S(1)} %copy-done), channel_id=1, source_target_pairs={{0,6},{1,7},{2,0},{3,1},{4,2},{5,3},{6,4},{7,5},{8,14},{9,15},{10,... | collective-permute-start | bytes 1572872 | tf_op jit(solution)/shard_map/ppermute | solution.py:45
  50.8 4.5 %collective-permute-start.4 = (bf16[4,128,2048]{2,1,0:T(8,128)(2,1)}, bf16[4,128,2048]{2,1,0:T(8,128)(2,1)}, u32[]{:S(2)}, u32[]{:S(2)}) collective-permute-start(bf16[4,128,2048]{2,1,0:T(8,128)(2,1)} %pad_maximum_fusion), channel_id=1, source_target_pairs={{0,1},{1,0},{2,3},{3,2},{4,5},{5,4},{6,7},{7,6},{8,9},{9,8},{10,11... | collective-permute-start | bytes 6291464 | tf_op jit(solution)/shard_map/ppermute | solution.py:40
  69.5 28.7 %collective-permute-start.5 = (bf16[2048,512]{1,0:T(8,128)(2,1)}, bf16[2048,512]{1,0:T(8,128)(2,1)S(1)}, u32[]{:S(2)}, u32[]{:S(2)}) collective-permute-start(bf16[2048,512]{1,0:T(8,128)(2,1)} %all-gather.4.cloned.1.call-done.pair_0), channel_id=1, source_target_pairs={{0,1},{1,0},{2,3},{3,2},{4,5},{5,4},{6,7},{7,6},{8,9},{9,8},{10,11... | collective-permute-start | bytes 6291464 | tf_op jit(solution)/shard_map/ppermute | solution.py:40
  70.8 27.3 %collective-permute-start.6 = (bf16[2048,256]{1,0:T(8,128)(2,1)S(1)}, bf16[2048,256]{1,0:T(8,128)(2,1)S(1)}, u32[]{:S(2)}, u32[]{:S(2)}) collective-permute-start(bf16[2048,256]{1,0:T(8,128)(2,1)S(1)} %slice.19), channel_id=1, source_target_pairs={{0,2},{1,3},{2,4},{3,5},{4,6},{5,7},{6,0},{7,1},{8,10},{9,11},{10,... | collective-permute-start | bytes 3145736 | tf_op jit(solution)/shard_map/ppermute | solution.py:45
  72.5 25.7 %collective-permute-start.7 = (bf16[2048,256]{1,0:T(8,128)(2,1)S(1)}, bf16[2048,256]{1,0:T(8,128)(2,1)S(1)}, u32[]{:S(2)}, u32[]{:S(2)}) collective-permute-start(bf16[2048,256]{1,0:T(8,128)(2,1)S(1)} %slice.19), channel_id=1, source_target_pairs={{0,6},{1,7},{2,0},{3,1},{4,2},{5,3},{6,4},{7,5},{8,14},{9,15},{10,... | collective-permute-start | bytes 3145736 | tf_op jit(solution)/shard_map/ppermute | solution.py:45
  98.2 34.3 %copy-start.9 = (bf16[2048,256]{1,0:T(8,128)(2,1)}, bf16[2048,256]{1,0:T(8,128)(2,1)S(1)}, u32[]{:S(2)}) copy-start(bf16[2048,256]{1,0:T(8,128)(2,1)S(1)} %collective-permute-done.6.near_0) | copy-start | bytes 3145732
  98.2 34.3 %copy-start.10 = (bf16[2048,256]{1,0:T(8,128)(2,1)}, bf16[2048,256]{1,0:T(8,128)(2,1)S(1)}, u32[]{:S(2)}) copy-start(bf16[2048,256]{1,0:T(8,128)(2,1)S(1)} %collective-permute-done.7.far_0) | copy-start | bytes 3145732
  98.2 34.3 %copy-start.8 = (bf16[2048,512]{1,0:T(8,128)(2,1)}, bf16[2048,512]{1,0:T(8,128)(2,1)S(1)}, u32[]{:S(2)}) copy-start(bf16[2048,512]{1,0:T(8,128)(2,1)S(1)} %collective-permute-done.5.pair_1) | copy-start | bytes 6291460
  98.2 34.3 %collective-permute-start.10 = (bf16[512,256]{1,0:T(8,128)(2,1)S(1)}, bf16[512,256]{1,0:T(8,128)(2,1)S(1)}, u32[]{:S(2)}, u32[]{:S(2)}) collective-permute-start(bf16[512,256]{1,0:T(8,128)(2,1)S(1)} %attention.2), channel_id=1, source_target_pairs={{0,6},{1,7},{2,0},{3,1},{4,2},{5,3},{6,4},{7,5},{8,14},{9,15},{10,... | collective-permute-start | bytes 786440 | tf_op jit(solution)/shard_map/ppermute | solution.py:45
  100.8 31.8 %collective-permute-start.8 = (bf16[512,256]{1,0:T(8,128)(2,1)S(1)}, bf16[512,256]{1,0:T(8,128)(2,1)S(1)}, u32[]{:S(2)}, u32[]{:S(2)}) collective-permute-start(bf16[512,256]{1,0:T(8,128)(2,1)S(1)} %attention.2), channel_id=1, source_target_pairs={{0,2},{1,3},{2,4},{3,5},{4,6},{5,7},{6,0},{7,1},{8,10},{9,11},{10,... | collective-permute-start | bytes 786440 | tf_op jit(solution)/shard_map/ppermute | solution.py:45
  100.8 31.8 %collective-permute-start.9 = (bf16[512,256]{1,0:T(8,128)(2,1)S(1)}, bf16[512,256]{1,0:T(8,128)(2,1)S(1)}, u32[]{:S(2)}, u32[]{:S(2)}) collective-permute-start(bf16[512,256]{1,0:T(8,128)(2,1)S(1)} %attention.2), channel_id=1, source_target_pairs={{0,4},{1,5},{2,6},{3,7},{4,0},{5,1},{6,2},{7,3},{8,12},{9,13},{10,... | collective-permute-start | bytes 786440 | tf_op jit(solution)/shard_map/ppermute | solution.py:45
  102.7 32.3 %collective-permute-start.11 = (bf16[2048,256]{1,0:T(8,128)(2,1)S(1)}, bf16[2048,256]{1,0:T(8,128)(2,1)S(1)}, u32[]{:S(2)}, u32[]{:S(2)}) collective-permute-start(bf16[2048,256]{1,0:T(8,128)(2,1)S(1)} %collective-permute-done.6.near_0), channel_id=1, source_target_pairs={{0,1},{1,0},{2,3},{3,2},{4,5},{5,4},{6,7},{7,6},{8,9},{9,8},{10,11... | collective-permute-start | bytes 3145736 | tf_op jit(solution)/shard_map/ppermute | solution.py:40
  102.7 34.9 %collective-permute-start.12 = (bf16[2048,256]{1,0:T(8,128)(2,1)S(1)}, bf16[2048,256]{1,0:T(8,128)(2,1)S(1)}, u32[]{:S(2)}, u32[]{:S(2)}) collective-permute-start(bf16[2048,256]{1,0:T(8,128)(2,1)S(1)} %collective-permute-done.7.far_0), channel_id=1, source_target_pairs={{0,1},{1,0},{2,3},{3,2},{4,5},{5,4},{6,7},{7,6},{8,9},{9,8},{10,11... | collective-permute-start | bytes 3145736 | tf_op jit(solution)/shard_map/ppermute | solution.py:40
  132.7 4.9 %collective-permute-start.13 = (bf16[4,512,256]{2,1,0:T(8,128)(2,1)S(1)}, bf16[4,512,256]{2,1,0:T(8,128)(2,1)S(1)}, u32[]{:S(2)}, u32[]{:S(2)}) collective-permute-start(bf16[4,512,256]{2,1,0:T(8,128)(2,1)S(1)} %pad_maximum_fusion.1.a_same), channel_id=1, source_target_pairs={{0,1},{1,0},{2,3},{3,2},{4,5},{5,4},{6,7},{7,6},{8,9},{9,8},{10,11... | collective-permute-start | bytes 3145736 | tf_op jit(solution)/shard_map/ppermute | solution.py:40
  132.8 16.4 %collective-permute-start.14 = (bf16[512,256]{1,0:T(8,128)(2,1)S(1)}, bf16[512,256]{1,0:T(8,128)(2,1)S(1)}, u32[]{:S(2)}, u32[]{:S(2)}) collective-permute-start(bf16[512,256]{1,0:T(8,128)(2,1)S(1)} %attention.3), channel_id=1, source_target_pairs={{0,2},{1,3},{2,4},{3,5},{4,6},{5,7},{6,0},{7,1},{8,10},{9,11},{10,... | collective-permute-start | bytes 786440 | tf_op jit(solution)/shard_map/ppermute | solution.py:45
  134.8 14.4 %collective-permute-start.15 = (bf16[512,256]{1,0:T(8,128)(2,1)S(1)}, bf16[512,256]{1,0:T(8,128)(2,1)S(1)}, u32[]{:S(2)}, u32[]{:S(2)}) collective-permute-start(bf16[512,256]{1,0:T(8,128)(2,1)S(1)} %attention.3), channel_id=1, source_target_pairs={{0,4},{1,5},{2,6},{3,7},{4,0},{5,1},{6,2},{7,3},{8,12},{9,13},{10,... | collective-permute-start | bytes 786440 | tf_op jit(solution)/shard_map/ppermute | solution.py:45
  135.0 14.3 %collective-permute-start.16 = (bf16[512,256]{1,0:T(8,128)(2,1)S(1)}, bf16[512,256]{1,0:T(8,128)(2,1)S(1)}, u32[]{:S(2)}, u32[]{:S(2)}) collective-permute-start(bf16[512,256]{1,0:T(8,128)(2,1)S(1)} %attention.3), channel_id=1, source_target_pairs={{0,6},{1,7},{2,0},{3,1},{4,2},{5,3},{6,4},{7,5},{8,14},{9,15},{10,... | collective-permute-start | bytes 786440 | tf_op jit(solution)/shard_map/ppermute | solution.py:45
  149.4 2.7 %collective-permute-start.17 = (bf16[4,512,256]{2,1,0:T(8,128)(2,1)S(1)}, bf16[4,512,256]{2,1,0:T(8,128)(2,1)S(1)}, u32[]{:S(2)}, u32[]{:S(2)}) collective-permute-start(bf16[4,512,256]{2,1,0:T(8,128)(2,1)S(1)} %pad_maximum_fusion.2.a_same), channel_id=1, source_target_pairs={{0,1},{1,0},{2,3},{3,2},{4,5},{5,4},{6,7},{7,6},{8,9},{9,8},{10,11... | collective-permute-start | bytes 3145736 | tf_op jit(solution)/shard_map/ppermute | solution.py:40
  171.0 8.1 %collective-permute-start.22 = (bf16[4,64,2048]{2,1,0:T(8,128)(2,1)}, bf16[4,64,2048]{2,1,0:T(8,128)(2,1)}, u32[]{:S(2)}, u32[]{:S(2)}) collective-permute-start(bf16[4,64,2048]{2,1,0:T(8,128)(2,1)} %get-tuple-element.70), channel_id=1, source_target_pairs={{0,1},{1,0},{2,3},{3,2},{4,5},{5,4},{6,7},{7,6},{8,9},{9,8},{10,11... | collective-permute-start | bytes 3145736 | tf_op jit(solution)/shard_map/ppermute | solution.py:40
  178.7 6.8 %collective-permute-start.18 = (bf16[4,64,2048]{2,1,0:T(8,128)(2,1)S(1)}, bf16[4,64,2048]{2,1,0:T(8,128)(2,1)}, u32[]{:S(2)}, u32[]{:S(2)}) collective-permute-start(bf16[4,64,2048]{2,1,0:T(8,128)(2,1)S(1)} %get-tuple-element.68), channel_id=1, source_target_pairs={{0,1},{1,0},{2,3},{3,2},{4,5},{5,4},{6,7},{7,6},{8,9},{9,8},{10,11... | collective-permute-start | bytes 3145736 | tf_op jit(solution)/shard_map/ppermute | solution.py:40
  180.8 10.2 %collective-permute-start.23 = (bf16[64,2048]{1,0:T(8,128)(2,1)S(1)}, bf16[64,2048]{1,0:T(8,128)(2,1)S(1)}, u32[]{:S(2)}, u32[]{:S(2)}) collective-permute-start(bf16[64,2048]{1,0:T(8,128)(2,1)S(1)} %get-tuple-element.77), channel_id=1, source_target_pairs={{0,2},{1,3},{2,4},{3,5},{4,6},{5,7},{6,0},{7,1},{8,10},{9,11},{10,... | collective-permute-start | bytes 786440 | tf_op jit(solution)/shard_map/ppermute | solution.py:45
  182.2 15.3 %collective-permute-start.24 = (bf16[64,2048]{1,0:T(8,128)(2,1)S(1)}, bf16[64,2048]{1,0:T(8,128)(2,1)S(1)}, u32[]{:S(2)}, u32[]{:S(2)}) collective-permute-start(bf16[64,2048]{1,0:T(8,128)(2,1)S(1)} %get-tuple-element.79), channel_id=1, source_target_pairs={{0,4},{1,5},{2,6},{3,7},{4,0},{5,1},{6,2},{7,3},{8,12},{9,13},{10,... | collective-permute-start | bytes 786440 | tf_op jit(solution)/shard_map/ppermute | solution.py:45
  184.7 13.2 %collective-permute-start.25 = (bf16[64,2048]{1,0:T(8,128)(2,1)S(1)}, bf16[64,2048]{1,0:T(8,128)(2,1)S(1)}, u32[]{:S(2)}, u32[]{:S(2)}) collective-permute-start(bf16[64,2048]{1,0:T(8,128)(2,1)S(1)} %get-tuple-element.78), channel_id=1, source_target_pairs={{0,6},{1,7},{2,0},{3,1},{4,2},{5,3},{6,4},{7,5},{8,14},{9,15},{10,... | collective-permute-start | bytes 786440 | tf_op jit(solution)/shard_map/ppermute | solution.py:45
  187.2 14.8 %collective-permute-start.19 = (bf16[64,2048]{1,0:T(8,128)(2,1)S(1)}, bf16[64,2048]{1,0:T(8,128)(2,1)S(1)}, u32[]{:S(2)}, u32[]{:S(2)}) collective-permute-start(bf16[64,2048]{1,0:T(8,128)(2,1)S(1)} %get-tuple-element.74), channel_id=1, source_target_pairs={{0,2},{1,3},{2,4},{3,5},{4,6},{5,7},{6,0},{7,1},{8,10},{9,11},{10,... | collective-permute-start | bytes 786440 | tf_op jit(solution)/shard_map/ppermute | solution.py:45
  188.5 19.5 %collective-permute-start.20 = (bf16[64,2048]{1,0:T(8,128)(2,1)S(1)}, bf16[64,2048]{1,0:T(8,128)(2,1)}, u32[]{:S(2)}, u32[]{:S(2)}) collective-permute-start(bf16[64,2048]{1,0:T(8,128)(2,1)S(1)} %get-tuple-element.76), channel_id=1, source_target_pairs={{0,4},{1,5},{2,6},{3,7},{4,0},{5,1},{6,2},{7,3},{8,12},{9,13},{10,... | collective-permute-start | bytes 786440 | tf_op jit(solution)/shard_map/ppermute | solution.py:45
  191.1 17.0 %collective-permute-start.21 = (bf16[64,2048]{1,0:T(8,128)(2,1)S(1)}, bf16[64,2048]{1,0:T(8,128)(2,1)}, u32[]{:S(2)}, u32[]{:S(2)}) collective-permute-start(bf16[64,2048]{1,0:T(8,128)(2,1)S(1)} %get-tuple-element.75), channel_id=1, source_target_pairs={{0,6},{1,7},{2,0},{3,1},{4,2},{5,3},{6,4},{7,5},{8,14},{9,15},{10,... | collective-permute-start | bytes 786440 | tf_op jit(solution)/shard_map/ppermute | solution.py:45
  (10 other events, 77.8 us)
Sparse Core Ops, SparseCore 0:
  10.7 58.7 all-gather.3
  71.7 71.1 all-gather.5

commit v2 on v1

--- a/solution.py
+++ b/solution.py
@@ -104,13 +104,13 @@
 
 
 def prepare_kernel(
-    lens_ref, part_ref, src_ref, gain_ref, cos_ref, sin_ref, w_ref, x_0, x_1, x_2, x_3, x_others,
+    lens_ref, part_ref, src_ref, gain_ref, cos_ref, sin_ref, w_ref, x_0, x_1, x_2, x_3, x_4, x_5, x_6, x_7,
     own_hbm, other_hbm, qt_hbm, kv_hbm, cache_hbm, rows_hbm, x_ref, kv_ref, new_ref, qt_ref, x_sems, load_sems, store_sems,
 ):
     req_count, block_pos, lanes = own_hbm.shape
     heads_dev = qt_ref.shape[2] // S_NEW
     half = HEAD_DIM // 2
-    x_pieces = [x_0, x_1, x_2, x_3] + [x_others.at[i] for i in range(Z)]
+    x_pieces = [x_0, x_1, x_2, x_3, x_4, x_5, x_6, x_7]
     piece_rows = x_0.shape[0]
     own_at = pl.multiple_of(part_ref[0] * block_pos, ALIGN)
     other_at = pl.multiple_of((1 - part_ref[0]) * block_pos, ALIGN)
@@ -223,7 +223,7 @@
             pltpu.HBM(own.shape, jnp.bfloat16),
             pltpu.HBM((rows, width), jnp.bfloat16),
         ),
-        in_specs=[scalar] * 3 + [whole] * 4 + [remote] * (Z + 3),
+        in_specs=[scalar] * 3 + [whole] * 4 + [remote] * (2 * Z + 2),
         out_specs=(pl.BlockSpec(memory_space=pltpu.HBM),) * 4,
         scratch_shapes=[
             pltpu.VMEM((rows, width), jnp.bfloat16),
@@ -239,7 +239,7 @@
             flops=4 * 10**9, transcendentals=10**6, bytes_accessed=20 * 10**6
         ),
         name="prepare",
-    )(lens, part, src, gain, cosine, sine, w, *x_same, x_others, in_hbm(own), other)
+    )(lens, part, src, gain, cosine, sine, w, *x_same, *x_others, in_hbm(own), other)
 
 
 def attention_kernel(which_ref, qt_hbm, kv_hbm, out_ref, qt_ref, kv_ref, acc_ref, top_ref, sems):
@@ -473,10 +473,15 @@
         ),
         "tok", axis=0, tiled=True,
     )
-    x_others = exchange(jnp.stack(x_same))
-    ff_part, group_w, other, *_ = lax.optimization_barrier(
-        (jnp.concatenate([w_gate.T, w_up.T, w_down], axis=0), group_w, other, *x_same)
-    )
+    x_others = [exchange(x_same[d]) if d != half_z else None for d in range(Z)]
+    early = [x_others[d] for d in range(Z) if d != half_z]
+    ff_part, group_w, other, x_same[half_z], *early = lax.optimization_barrier(
+        (
+            jnp.concatenate([w_gate.T, w_up.T, w_down], axis=0),
+            group_w, other, x_same[half_z], *early,
+        )
+    )
+    x_others = early[:half_z] + [exchange(x_same[half_z])] + early[half_z:]
     ff_weights = lax.all_gather(ff_part, "tok", axis=0)
     cosine, sine = angles_of(cached_len)
     qt, kv, cache_new, rows = prepare(

time: 219 us -> 220 us (level)
  waiting for transfers between devices: 45.1 us -> 56.7 us
  Pallas kernels: 99.8 us -> 94.8 us
  other arithmetic: 14.5 us -> 11.8 us
  starting transfers between devices: 36.3 us -> 33.7 us
    ppermute x17, waiting for transfers between devices: 36.4 us -> 45.8 us  [along_z(): lax.ppermute(array, 'head', [(i, (i + 2 * distance) % count) for i in ran...]
    pallas_call x2, Pallas kernels: 53.3 us -> 48.3 us  [attention(): pl.pallas_call(attention_kernel, out_shape=jax.ShapeDtypeStruct((S_NEW, c...]
    all_gather x1, waiting for transfers between devices: 4.35 us -> 8.1 us  [per_device(): lax.all_gather(jnp.concatenate([lax.dynamic_slice_in_dim(w_out, block * o...]
    ppermute x17, starting transfers between devices: 27.5 us -> 24.4 us  [along_z(): lax.ppermute(array, 'head', [(i, (i + 2 * distance) % count) for i in ran...]
    another operation x1 -> x0, other arithmetic: 2.63 us -> none  [per_device(): x_others = exchange(jnp.stack(x_same))]
  transfers between devices with their start and end apart: 29 -> 32, of which waited for: 11 -> 11; matrix products, arithmetic and copies ran while one was open for 8% -> 6% of each run, Pallas kernels for 37% -> 35%
where the time goes in v2:
time: 220 us; the launch traced here: 219 us
  Pallas kernels  94.8 us (43%)
  waiting for transfers between devices  56.7 us (26%)
  starting transfers between devices  33.7 us (15%)
  between operations  14.5 us (7%)
  other arithmetic  11.8 us (5%)
  local copies, waits for them, and re-layouts  7.68 us (3%)
    pallas_call x2, Pallas kernels, attention(): pl.pallas_call(attention_kernel, out_shape=jax.ShapeDtypeStruct((S_NEW, c...  48.3 us
    ppermute x17, waiting for transfers between devices, along_z(): lax.ppermute(array, 'head', [(i, (i + 2 * distance) % count) for i in ran...  45.8 us
    ppermute x17, starting transfers between devices, along_z(): lax.ppermute(array, 'head', [(i, (i + 2 * distance) % count) for i in ran...  24.4 us
    pallas_call x2, Pallas kernels, project_out(): pl.pallas_call(out_kernel, out_shape=(pltpu.HBM((piece_rows, width), jnp....  21.1 us
    pallas_call x2, Pallas kernels, feed_forward(): pl.pallas_call(ff_kernel, out_shape=(jax.ShapeDtypeStruct((Z, rows, width...  15.4 us
    pallas_call x1, Pallas kernels, prepare(): pl.pallas_call(prepare_kernel, out_shape=(pltpu.HBM((req_count, lanes, he...  10 us
    all_gather x1, waiting for transfers between devices, per_device(): lax.all_gather(jnp.concatenate([lax.dynamic_slice_in_dim(w_out, block * o...  8.1 us
    all_to_all x1, starting transfers between devices, per_device(): lax.all_to_all(spread, 'tok', 0, 0, tiled=True)  7.25 us
  transfers between devices with their start and end apart: 32, of which 11 were waited for; matrix products, arithmetic and copies ran while one was open for 6% of the time, Pallas kernels for 35%

profile of v2, /device:TPU:0, one launch (start us, length us, event | category | flops | bytes accessed | tf_op | source)
XLA Modules:
  0.0 219.2 jit_solution(9203202878761003151)
XLA Ops:
  12.1 7.2 %all-to-all-start = ((bf16[16,128,384]{2,1,0:T(8,128)(2,1)}), bf16[16,128,384]{2,1,0:T(8,128)(2,1)S(1)}, u32[]{:S(2)}, u32[]{:S(2)}) async-start(bf16[16,128,384]{2,1,0:T(8,128)(2,1)} %broadcast_in_dim.9), calls=%async_computation | async-start | bytes 3145728 | tf_op jit(solution)/shard_map/all_to_all | solution.py:463
  19.4 2.0 collective-permute-start.3
  21.4 2.2 %collective-permute-start.5 = (bf16[128,2048]{1,0:T(8,128)(2,1)S(1)}, bf16[128,2048]{1,0:T(8,128)(2,1)S(1)}, u32[]{:S(2)}, u32[]{:S(2)}) collective-permute-start(bf16[128,2048]{1,0:T(8,128)(2,1)S(1)} %copy-done.2), channel_id=1, source_target_pairs={{0,6},{1,7},{2,0},{3,1},{4,2},{5,3},{6,4},{7,5},{8,14},{9,15},{10,... | collective-permute-start | bytes 1572872 | tf_op jit(solution)/shard_map/ppermute | solution.py:45
  23.6 1.8 collective-permute-start.1
  25.4 10.4 %collective-permute-done.3.x_1 = bf16[128,2048]{1,0:T(8,128)(2,1)S(1)} collective-permute-done((bf16[128,2048]{1,0:T(8,128)(2,1)S(1)}, bf16[128,2048]{1,0:T(8,128)(2,1)S(1)}, u32[]{:S(2)}, u32[]{:S(2)}) %collective-permute-start.3) | collective-permute-done | bytes 524320 | tf_op jit(solution)/shard_map/ppermute | solution.py:45
  35.8 10.6 %collective-permute-done.5.x_3 = bf16[128,2048]{1,0:T(8,128)(2,1)S(1)} collective-permute-done((bf16[128,2048]{1,0:T(8,128)(2,1)S(1)}, bf16[128,2048]{1,0:T(8,128)(2,1)S(1)}, u32[]{:S(2)}, u32[]{:S(2)}) %collective-permute-start.5) | collective-permute-done | bytes 524320 | tf_op jit(solution)/shard_map/ppermute | solution.py:45
  46.4 1.8 pad_maximum_fusion.2
  51.5 10.0 %prepare.1 = (bf16[2,128,2048]{2,1,0:T(8,128)(2,1)}, bf16[2,8720,128]{2,1,0:T(8,128)(2,1)}, bf16[2,4352,128]{2,1,0:T(8,128)(2,1)}, bf16[1024,2048]{1,0:T(8,128)(2,1)}) custom-call(s32[2]{0:T(128)S(1)} %copy-done, s32[1]{0:T(128)} %bitcast.part_ref, s32[8]{0:T(128)S(1)} %pad_add_fusion.4.src_ref, f32[1,2048]{1,0:T(1,128)S(1)} %bitcast.59, ...), custom_call_target="tpu_custom_call" | custom-call | flops 4000000000 | bytes 20000000 | tf_op jit(solution)/shard_map/prepare/pallas_call | solution.py:218
  61.5 8.1 %all-gather.4.cloned.1.call-done.pair_0 = bf16[2048,512]{1,0:T(8,128)(2,1)} async-done(((bf16[128,512]{1,0:T(8,128)(2,1)}), bf16[2048,512]{1,0:T(8,128)(2,1)}) %all-gather.4.cloned.1.call-update) | async-done | bytes 2097168 | tf_op jit(solution)/shard_map/all_gather | solution.py:466
  69.7 1.4 slice.19
  71.6 2.9 %collective-permute-start.10 = (bf16[2048,256]{1,0:T(8,128)(2,1)S(1)}, bf16[2048,256]{1,0:T(8,128)(2,1)S(1)}, u32[]{:S(2)}, u32[]{:S(2)}) collective-permute-start(bf16[2048,256]{1,0:T(8,128)(2,1)S(1)} %slice.19), channel_id=1, source_target_pairs={{0,6},{1,7},{2,0},{3,1},{4,2},{5,3},{6,4},{7,5},{8,14},{9,15},{10,... | collective-permute-start | bytes 3145736 | tf_op jit(solution)/shard_map/ppermute | solution.py:45
  74.5 19.7 %attention.2 = bf16[512,256]{1,0:T(8,128)(2,1)S(1)} custom-call(s32[2]{0:T(128)S(1)} %pad_add_fusion.3.which_ref, bf16[2,128,2048]{2,1,0:T(8,128)(2,1)} %get-tuple-element.53.qt_hbm, bf16[2,8720,128]{2,1,0:T(8,128)(2,1)} %get-tuple-element.51.kv_hbm), custom_call_target="tpu_custom_call" | custom-call | flops 40000000000 | bytes 100000000 | tf_op jit(solution)/shard_map/attention/pallas_call | solution.py:260
  94.2 3.4 %collective-permute-done.10.far_0 = bf16[2048,256]{1,0:T(8,128)(2,1)S(1)} collective-permute-done((bf16[2048,256]{1,0:T(8,128)(2,1)S(1)}, bf16[2048,256]{1,0:T(8,128)(2,1)S(1)}, u32[]{:S(2)}, u32[]{:S(2)}) %collective-permute-start.10) | collective-permute-done | bytes 1048608 | tf_op jit(solution)/shard_map/ppermute | solution.py:45
  97.6 3.4 %collective-permute-done.9.near_0 = bf16[2048,256]{1,0:T(8,128)(2,1)S(1)} collective-permute-done((bf16[2048,256]{1,0:T(8,128)(2,1)S(1)}, bf16[2048,256]{1,0:T(8,128)(2,1)S(1)}, u32[]{:S(2)}, u32[]{:S(2)}) %collective-permute-start.9) | collective-permute-done | bytes 1048608 | tf_op jit(solution)/shard_map/ppermute | solution.py:45
  101.1 1.7 collective-permute-start.12
  102.9 1.5 collective-permute-start.13
  104.9 28.6 %attention.3 = bf16[512,256]{1,0:T(8,128)(2,1)S(1)} custom-call(s32[2]{0:T(128)S(1)} %pad_add_fusion.1.which_ref, bf16[2,128,2048]{2,1,0:T(8,128)(2,1)} %get-tuple-element.53.qt_hbm, bf16[2,8720,128]{2,1,0:T(8,128)(2,1)} %get-tuple-element.51.kv_hbm), custom_call_target="tpu_custom_call" | custom-call | flops 40000000000 | bytes 100000000 | tf_op jit(solution)/shard_map/attention/pallas_call | solution.py:260
  135.1 1.9 collective-permute-start.18
  137.1 2.6 %collective-permute-start.19 = (bf16[512,256]{1,0:T(8,128)(2,1)S(1)}, bf16[512,256]{1,0:T(8,128)(2,1)S(1)}, u32[]{:S(2)}, u32[]{:S(2)}) collective-permute-start(bf16[512,256]{1,0:T(8,128)(2,1)S(1)} %attention.3), channel_id=1, source_target_pairs={{0,6},{1,7},{2,0},{3,1},{4,2},{5,3},{6,4},{7,5},{8,14},{9,15},{10,... | collective-permute-start | bytes 786440 | tf_op jit(solution)/shard_map/ppermute | solution.py:45
  140.7 10.6 %project_out.2 = (bf16[512,2048]{1,0:T(8,128)(2,1)}, bf16[512,2048]{1,0:T(8,128)(2,1)}) custom-call(s32[8]{0:T(128)S(1)} %pad_add_fusion.4.src_ref, s32[1]{0:T(128)} %constant.121.clone.1.request_ref, f32[1,2048]{1,0:T(1,128)S(1)} %bitcast.60, bf16[1024,2048]{1,0:T(8,128)(2,1)} %get-tuple-element.56.rows_hbm, ...), custom_call_target="tpu_custom_call" | custom-call | flops 4000000000 | bytes 16000000 | tf_op jit(solution)/shard_map/project_out/pallas_call | solution.py:332
  151.6 2.6 %collective-permute-done.20.a_others = bf16[4,512,256]{2,1,0:T(8,128)(2,1)S(1)} collective-permute-done((bf16[4,512,256]{2,1,0:T(8,128)(2,1)S(1)}, bf16[4,512,256]{2,1,0:T(8,128)(2,1)S(1)}, u32[]{:S(2)}, u32[]{:S(2)}) %collective-permute-start.20) | collective-permute-done | bytes 1048608 | tf_op jit(solution)/shard_map/ppermute | solution.py:40
  154.2 10.5 %project_out.3 = (bf16[512,2048]{1,0:T(8,128)(2,1)}, bf16[512,2048]{1,0:T(8,128)(2,1)}) custom-call(s32[8]{0:T(128)S(1)} %pad_add_fusion.4.src_ref, s32[1]{0:T(128)} %constant.120.clone.1.request_ref, f32[1,2048]{1,0:T(1,128)S(1)} %bitcast.61, bf16[1024,2048]{1,0:T(8,128)(2,1)} %get-tuple-element.56.rows_hbm, ...), custom_call_target="tpu_custom_call" | custom-call | flops 4000000000 | bytes 16000000 | tf_op jit(solution)/shard_map/project_out/pallas_call | solution.py:332
  164.7 8.2 %feed_forward.3 = (bf16[4,64,2048]{2,1,0:T(8,128)(2,1)S(1)}, bf16[4,64,2048]{2,1,0:T(8,128)(2,1)}) custom-call(s32[2]{0:T(128)S(1)} %get-tuple-element.98.place_ref, bf16[4,128,2048]{2,1,0:T(8,128)(2,1)} %bitcast.76, bf16[4,128,2048]{2,1,0:T(8,128)(2,1)} %bitcast.78, bf16[16,2112,128]{2,1,0:T(8,128)(2,1)S(1)} %bitcast.57), custom_call_target="tpu_custom_call" | custom-call | flops 5000000000 | bytes 16000000 | tf_op jit(solution)/shard_map/feed_forward/pallas_call | solution.py:409
  173.3 7.2 %feed_forward.2 = (bf16[4,64,2048]{2,1,0:T(8,128)(2,1)S(1)}, bf16[4,64,2048]{2,1,0:T(8,128)(2,1)S(1)}) custom-call(s32[2]{0:T(128)S(1)} %get-tuple-element.99.place_ref, bf16[4,128,2048]{2,1,0:T(8,128)(2,1)} %bitcast.77, bf16[4,128,2048]{2,1,0:T(8,128)(2,1)} %bitcast.79, bf16[16,2112,128]{2,1,0:T(8,128)(2,1)S(1)} %bitcast.58), custom_call_target="tpu_custom_call" | custom-call | flops 5000000000 | bytes 16000000 | tf_op jit(solution)/shard_map/feed_forward/pallas_call | solution.py:409
  181.0 1.6 add_convert_fusion
  183.2 2.4 %collective-permute-start.27 = (bf16[64,2048]{1,0:T(8,128)(2,1)S(1)}, bf16[64,2048]{1,0:T(8,128)(2,1)S(1)}, u32[]{:S(2)}, u32[]{:S(2)}) collective-permute-start(bf16[64,2048]{1,0:T(8,128)(2,1)S(1)} %get-tuple-element.87), channel_id=1, source_target_pairs={{0,4},{1,5},{2,6},{3,7},{4,0},{5,1},{6,2},{7,3},{8,12},{9,13},{10,... | collective-permute-start | bytes 786440 | tf_op jit(solution)/shard_map/ppermute | solution.py:45
  185.6 1.6 collective-permute-start.28
  187.2 1.6 add_convert_fusion.1
  189.4 1.5 collective-permute-start.23
  190.9 7.8 %collective-permute-done.26 = bf16[64,2048]{1,0:T(8,128)(2,1)S(1)} collective-permute-done((bf16[64,2048]{1,0:T(8,128)(2,1)S(1)}, bf16[64,2048]{1,0:T(8,128)(2,1)S(1)}, u32[]{:S(2)}, u32[]{:S(2)}) %collective-permute-start.26) | collective-permute-done | bytes 262176 | tf_op jit(solution)/shard_map/ppermute | solution.py:45
  200.0 9.2 %collective-permute-done.22 = bf16[64,2048]{1,0:T(8,128)(2,1)S(1)} collective-permute-done((bf16[64,2048]{1,0:T(8,128)(2,1)S(1)}, bf16[64,2048]{1,0:T(8,128)(2,1)S(1)}, u32[]{:S(2)}, u32[]{:S(2)}) %collective-permute-start.22) | collective-permute-done | bytes 262176 | tf_op jit(solution)/shard_map/ppermute | solution.py:45
  210.0 1.5 fusion.5
  (96 shorter events, 17.0 us)
Async XLA Ops:
  7.2 62.5 %all-gather.4.cloned.1.call-start = ((), (), s32[]{:S(2)}) async-start(), calls=%async_computation.1 | async-start | bytes 2228224 | tf_op jit(solution)/shard_map/all_gather | solution.py:466
  8.8 39.7 %collective-permute-start = (bf16[2,4352,128]{2,1,0:T(8,128)(2,1)}, bf16[2,4352,128]{2,1,0:T(8,128)(2,1)}, u32[]{:S(2)}, u32[]{:S(2)}) collective-permute-start(bf16[2,4352,128]{2,1,0:T(8,128)(2,1)} %bitcast.73), channel_id=1, source_target_pairs={{0,1},{1,0},{2,3},{3,2},{4,5},{5,4},{6,7},{7,6},{8,9},{9,8},{10,11... | collective-permute-start | bytes 6684680 | tf_op jit(solution)/shard_map/ppermute | solution.py:40
  12.1 36.3 %all-to-all-start = ((bf16[16,128,384]{2,1,0:T(8,128)(2,1)}), bf16[16,128,384]{2,1,0:T(8,128)(2,1)S(1)}, u32[]{:S(2)}, u32[]{:S(2)}) async-start(bf16[16,128,384]{2,1,0:T(8,128)(2,1)} %broadcast_in_dim.9), calls=%async_computation | async-start | bytes 3145728 | tf_op jit(solution)/shard_map/all_to_all | solution.py:463
  19.4 131.9 %all-gather.6.cloned.1.call-start = ((), (), s32[]{:S(2)}) async-start(), calls=%async_computation.2 | async-start | bytes 9191424 | tf_op jit(solution)/shard_map/all_gather | solution.py:485
  19.4 16.4 %collective-permute-start.3 = (bf16[128,2048]{1,0:T(8,128)(2,1)S(1)}, bf16[128,2048]{1,0:T(8,128)(2,1)S(1)}, u32[]{:S(2)}, u32[]{:S(2)}) collective-permute-start(bf16[128,2048]{1,0:T(8,128)(2,1)S(1)} %copy-done.2), channel_id=1, source_target_pairs={{0,2},{1,3},{2,4},{3,5},{4,6},{5,7},{6,0},{7,1},{8,10},{9,11},{10,... | collective-permute-start | bytes 1572872 | tf_op jit(solution)/shard_map/ppermute | solution.py:45
  21.4 25.0 %collective-permute-start.5 = (bf16[128,2048]{1,0:T(8,128)(2,1)S(1)}, bf16[128,2048]{1,0:T(8,128)(2,1)S(1)}, u32[]{:S(2)}, u32[]{:S(2)}) collective-permute-start(bf16[128,2048]{1,0:T(8,128)(2,1)S(1)} %copy-done.2), channel_id=1, source_target_pairs={{0,6},{1,7},{2,0},{3,1},{4,2},{5,3},{6,4},{7,5},{8,14},{9,15},{10,... | collective-permute-start | bytes 1572872 | tf_op jit(solution)/shard_map/ppermute | solution.py:45
  23.6 24.7 %collective-permute-start.1 = (bf16[128,2048]{1,0:T(8,128)(2,1)S(1)}, bf16[128,2048]{1,0:T(8,128)(2,1)}, u32[]{:S(2)}, u32[]{:S(2)}) collective-permute-start(bf16[128,2048]{1,0:T(8,128)(2,1)S(1)} %copy-done.2), channel_id=1, source_target_pairs={{0,4},{1,5},{2,6},{3,7},{4,0},{5,1},{6,2},{7,3},{8,12},{9,13},{10,... | collective-permute-start | bytes 1572872 | tf_op jit(solution)/shard_map/ppermute | solution.py:45
  25.4 22.9 %collective-permute-start.2 = (bf16[128,2048]{1,0:T(8,128)(2,1)S(1)}, bf16[128,2048]{1,0:T(8,128)(2,1)}, u32[]{:S(2)}, u32[]{:S(2)}) collective-permute-start(bf16[128,2048]{1,0:T(8,128)(2,1)S(1)} %copy-done.2), channel_id=1, source_target_pairs={{0,1},{1,0},{2,3},{3,2},{4,5},{5,4},{6,7},{7,6},{8,9},{9,8},{10,11... | collective-permute-start | bytes 1572872 | tf_op jit(solution)/shard_map/ppermute | solution.py:40
  35.8 12.5 %collective-permute-start.4 = (bf16[128,2048]{1,0:T(8,128)(2,1)S(1)}, bf16[128,2048]{1,0:T(8,128)(2,1)}, u32[]{:S(2)}, u32[]{:S(2)}) collective-permute-start(bf16[128,2048]{1,0:T(8,128)(2,1)S(1)} %collective-permute-done.3.x_1), channel_id=1, source_target_pairs={{0,1},{1,0},{2,3},{3,2},{4,5},{5,4},{6,7},{7,6},{8,9},{9,8},{10,11... | collective-permute-start | bytes 1572872 | tf_op jit(solution)/shard_map/ppermute | solution.py:40
  46.4 2.0 collective-permute-start.6
  49.2 2.3 %collective-permute-start.7 = (bf16[128,2048]{1,0:T(8,128)(2,1)}, bf16[128,2048]{1,0:T(8,128)(2,1)S(1)}, u32[]{:S(2)}, u32[]{:S(2)}) collective-permute-start(bf16[128,2048]{1,0:T(8,128)(2,1)} %collective-permute-done.1.x_2), channel_id=1, source_target_pairs={{0,1},{1,0},{2,3},{3,2},{4,5},{5,4},{6,7},{7,6},{8,9},{9,8},{10,11... | collective-permute-start | bytes 1572872 | tf_op jit(solution)/shard_map/ppermute | solution.py:40
  71.6 29.5 %collective-permute-start.8 = (bf16[2048,512]{1,0:T(8,128)(2,1)S(1)}, bf16[2048,512]{1,0:T(8,128)(2,1)S(1)}, u32[]{:S(2)}, u32[]{:S(2)}) collective-permute-start(bf16[2048,512]{1,0:T(8,128)(2,1)S(1)} %copy-done.6), channel_id=1, source_target_pairs={{0,1},{1,0},{2,3},{3,2},{4,5},{5,4},{6,7},{7,6},{8,9},{9,8},{10,11... | collective-permute-start | bytes 6291464 | tf_op jit(solution)/shard_map/ppermute | solution.py:40
  71.6 26.1 %collective-permute-start.10 = (bf16[2048,256]{1,0:T(8,128)(2,1)S(1)}, bf16[2048,256]{1,0:T(8,128)(2,1)S(1)}, u32[]{:S(2)}, u32[]{:S(2)}) collective-permute-start(bf16[2048,256]{1,0:T(8,128)(2,1)S(1)} %slice.19), channel_id=1, source_target_pairs={{0,6},{1,7},{2,0},{3,1},{4,2},{5,3},{6,4},{7,5},{8,14},{9,15},{10,... | collective-permute-start | bytes 3145736 | tf_op jit(solution)/shard_map/ppermute | solution.py:45
  74.5 26.5 %collective-permute-start.9 = (bf16[2048,256]{1,0:T(8,128)(2,1)S(1)}, bf16[2048,256]{1,0:T(8,128)(2,1)S(1)}, u32[]{:S(2)}, u32[]{:S(2)}) collective-permute-start(bf16[2048,256]{1,0:T(8,128)(2,1)S(1)} %slice.19), channel_id=1, source_target_pairs={{0,2},{1,3},{2,4},{3,5},{4,6},{5,7},{6,0},{7,1},{8,10},{9,11},{10,... | collective-permute-start | bytes 3145736 | tf_op jit(solution)/shard_map/ppermute | solution.py:45
  101.0 32.5 %collective-permute-start.11 = (bf16[512,256]{1,0:T(8,128)(2,1)S(1)}, bf16[512,256]{1,0:T(8,128)(2,1)S(1)}, u32[]{:S(2)}, u32[]{:S(2)}) collective-permute-start(bf16[512,256]{1,0:T(8,128)(2,1)S(1)} %attention.2), channel_id=1, source_target_pairs={{0,2},{1,3},{2,4},{3,5},{4,6},{5,7},{6,0},{7,1},{8,10},{9,11},{10,... | collective-permute-start | bytes 786440 | tf_op jit(solution)/shard_map/ppermute | solution.py:45
  101.1 32.4 %collective-permute-start.12 = (bf16[512,256]{1,0:T(8,128)(2,1)S(1)}, bf16[512,256]{1,0:T(8,128)(2,1)S(1)}, u32[]{:S(2)}, u32[]{:S(2)}) collective-permute-start(bf16[512,256]{1,0:T(8,128)(2,1)S(1)} %attention.2), channel_id=1, source_target_pairs={{0,4},{1,5},{2,6},{3,7},{4,0},{5,1},{6,2},{7,3},{8,12},{9,13},{10,... | collective-permute-start | bytes 786440 | tf_op jit(solution)/shard_map/ppermute | solution.py:45
  102.9 30.7 %collective-permute-start.13 = (bf16[512,256]{1,0:T(8,128)(2,1)S(1)}, bf16[512,256]{1,0:T(8,128)(2,1)S(1)}, u32[]{:S(2)}, u32[]{:S(2)}) collective-permute-start(bf16[512,256]{1,0:T(8,128)(2,1)S(1)} %attention.2), channel_id=1, source_target_pairs={{0,6},{1,7},{2,0},{3,1},{4,2},{5,3},{6,4},{7,5},{8,14},{9,15},{10,... | collective-permute-start | bytes 786440 | tf_op jit(solution)/shard_map/ppermute | solution.py:45
  104.3 32.7 %collective-permute-start.14 = (bf16[2048,256]{1,0:T(8,128)(2,1)S(1)}, bf16[2048,256]{1,0:T(8,128)(2,1)S(1)}, u32[]{:S(2)}, u32[]{:S(2)}) collective-permute-start(bf16[2048,256]{1,0:T(8,128)(2,1)S(1)} %collective-permute-done.9.near_0), channel_id=1, source_target_pairs={{0,1},{1,0},{2,3},{3,2},{4,5},{5,4},{6,7},{7,6},{8,9},{9,8},{10,11... | collective-permute-start | bytes 3145736 | tf_op jit(solution)/shard_map/ppermute | solution.py:40
  104.3 35.3 %collective-permute-start.15 = (bf16[2048,256]{1,0:T(8,128)(2,1)S(1)}, bf16[2048,256]{1,0:T(8,128)(2,1)S(1)}, u32[]{:S(2)}, u32[]{:S(2)}) collective-permute-start(bf16[2048,256]{1,0:T(8,128)(2,1)S(1)} %collective-permute-done.10.far_0), channel_id=1, source_target_pairs={{0,1},{1,0},{2,3},{3,2},{4,5},{5,4},{6,7},{7,6},{8,9},{9,8},{10,11... | collective-permute-start | bytes 3145736 | tf_op jit(solution)/shard_map/ppermute | solution.py:40
  133.7 5.9 %collective-permute-start.16 = (bf16[4,512,256]{2,1,0:T(8,128)(2,1)S(1)}, bf16[4,512,256]{2,1,0:T(8,128)(2,1)S(1)}, u32[]{:S(2)}, u32[]{:S(2)}) collective-permute-start(bf16[4,512,256]{2,1,0:T(8,128)(2,1)S(1)} %pad_maximum_fusion.a_same), channel_id=1, source_target_pairs={{0,1},{1,0},{2,3},{3,2},{4,5},{5,4},{6,7},{7,6},{8,9},{9,8},{10,11... | collective-permute-start | bytes 3145736 | tf_op jit(solution)/shard_map/ppermute | solution.py:40
  133.8 17.4 %collective-permute-start.17 = (bf16[512,256]{1,0:T(8,128)(2,1)S(1)}, bf16[512,256]{1,0:T(8,128)(2,1)S(1)}, u32[]{:S(2)}, u32[]{:S(2)}) collective-permute-start(bf16[512,256]{1,0:T(8,128)(2,1)S(1)} %attention.3), channel_id=1, source_target_pairs={{0,2},{1,3},{2,4},{3,5},{4,6},{5,7},{6,0},{7,1},{8,10},{9,11},{10,... | collective-permute-start | bytes 786440 | tf_op jit(solution)/shard_map/ppermute | solution.py:45
  135.1 16.1 %collective-permute-start.18 = (bf16[512,256]{1,0:T(8,128)(2,1)S(1)}, bf16[512,256]{1,0:T(8,128)(2,1)S(1)}, u32[]{:S(2)}, u32[]{:S(2)}) collective-permute-start(bf16[512,256]{1,0:T(8,128)(2,1)S(1)} %attention.3), channel_id=1, source_target_pairs={{0,4},{1,5},{2,6},{3,7},{4,0},{5,1},{6,2},{7,3},{8,12},{9,13},{10,... | collective-permute-start | bytes 786440 | tf_op jit(solution)/shard_map/ppermute | solution.py:45
  137.1 14.2 %collective-permute-start.19 = (bf16[512,256]{1,0:T(8,128)(2,1)S(1)}, bf16[512,256]{1,0:T(8,128)(2,1)S(1)}, u32[]{:S(2)}, u32[]{:S(2)}) collective-permute-start(bf16[512,256]{1,0:T(8,128)(2,1)S(1)} %attention.3), channel_id=1, source_target_pairs={{0,6},{1,7},{2,0},{3,1},{4,2},{5,3},{6,4},{7,5},{8,14},{9,15},{10,... | collective-permute-start | bytes 786440 | tf_op jit(solution)/shard_map/ppermute | solution.py:45
  151.4 2.7 %collective-permute-start.20 = (bf16[4,512,256]{2,1,0:T(8,128)(2,1)S(1)}, bf16[4,512,256]{2,1,0:T(8,128)(2,1)S(1)}, u32[]{:S(2)}, u32[]{:S(2)}) collective-permute-start(bf16[4,512,256]{2,1,0:T(8,128)(2,1)S(1)} %pad_maximum_fusion.1.a_same), channel_id=1, source_target_pairs={{0,1},{1,0},{2,3},{3,2},{4,5},{5,4},{6,7},{7,6},{8,9},{9,8},{10,11... | collective-permute-start | bytes 3145736 | tf_op jit(solution)/shard_map/ppermute | solution.py:40
  172.9 8.1 %collective-permute-start.25 = (bf16[4,64,2048]{2,1,0:T(8,128)(2,1)}, bf16[4,64,2048]{2,1,0:T(8,128)(2,1)}, u32[]{:S(2)}, u32[]{:S(2)}) collective-permute-start(bf16[4,64,2048]{2,1,0:T(8,128)(2,1)} %get-tuple-element.78), channel_id=1, source_target_pairs={{0,1},{1,0},{2,3},{3,2},{4,5},{5,4},{6,7},{7,6},{8,9},{9,8},{10,11... | collective-permute-start | bytes 3145736 | tf_op jit(solution)/shard_map/ppermute | solution.py:40
  180.6 6.6 %collective-permute-start.21 = (bf16[4,64,2048]{2,1,0:T(8,128)(2,1)S(1)}, bf16[4,64,2048]{2,1,0:T(8,128)(2,1)}, u32[]{:S(2)}, u32[]{:S(2)}) collective-permute-start(bf16[4,64,2048]{2,1,0:T(8,128)(2,1)S(1)} %get-tuple-element.76), channel_id=1, source_target_pairs={{0,1},{1,0},{2,3},{3,2},{4,5},{5,4},{6,7},{7,6},{8,9},{9,8},{10,11... | collective-permute-start | bytes 3145736 | tf_op jit(solution)/shard_map/ppermute | solution.py:40
  182.8 15.9 %collective-permute-start.26 = (bf16[64,2048]{1,0:T(8,128)(2,1)S(1)}, bf16[64,2048]{1,0:T(8,128)(2,1)S(1)}, u32[]{:S(2)}, u32[]{:S(2)}) collective-permute-start(bf16[64,2048]{1,0:T(8,128)(2,1)S(1)} %get-tuple-element.85), channel_id=1, source_target_pairs={{0,2},{1,3},{2,4},{3,5},{4,6},{5,7},{6,0},{7,1},{8,10},{9,11},{10,... | collective-permute-start | bytes 786440 | tf_op jit(solution)/shard_map/ppermute | solution.py:45
  183.2 16.8 %collective-permute-start.27 = (bf16[64,2048]{1,0:T(8,128)(2,1)S(1)}, bf16[64,2048]{1,0:T(8,128)(2,1)S(1)}, u32[]{:S(2)}, u32[]{:S(2)}) collective-permute-start(bf16[64,2048]{1,0:T(8,128)(2,1)S(1)} %get-tuple-element.87), channel_id=1, source_target_pairs={{0,4},{1,5},{2,6},{3,7},{4,0},{5,1},{6,2},{7,3},{8,12},{9,13},{10,... | collective-permute-start | bytes 786440 | tf_op jit(solution)/shard_map/ppermute | solution.py:45
  185.6 14.4 %collective-permute-start.28 = (bf16[64,2048]{1,0:T(8,128)(2,1)S(1)}, bf16[64,2048]{1,0:T(8,128)(2,1)S(1)}, u32[]{:S(2)}, u32[]{:S(2)}) collective-permute-start(bf16[64,2048]{1,0:T(8,128)(2,1)S(1)} %get-tuple-element.86), channel_id=1, source_target_pairs={{0,6},{1,7},{2,0},{3,1},{4,2},{5,3},{6,4},{7,5},{8,14},{9,15},{10,... | collective-permute-start | bytes 786440 | tf_op jit(solution)/shard_map/ppermute | solution.py:45
  188.9 20.3 %collective-permute-start.22 = (bf16[64,2048]{1,0:T(8,128)(2,1)S(1)}, bf16[64,2048]{1,0:T(8,128)(2,1)S(1)}, u32[]{:S(2)}, u32[]{:S(2)}) collective-permute-start(bf16[64,2048]{1,0:T(8,128)(2,1)S(1)} %get-tuple-element.82), channel_id=1, source_target_pairs={{0,2},{1,3},{2,4},{3,5},{4,6},{5,7},{6,0},{7,1},{8,10},{9,11},{10,... | collective-permute-start | bytes 786440 | tf_op jit(solution)/shard_map/ppermute | solution.py:45
  189.4 19.8 %collective-permute-start.23 = (bf16[64,2048]{1,0:T(8,128)(2,1)S(1)}, bf16[64,2048]{1,0:T(8,128)(2,1)}, u32[]{:S(2)}, u32[]{:S(2)}) collective-permute-start(bf16[64,2048]{1,0:T(8,128)(2,1)S(1)} %get-tuple-element.84), channel_id=1, source_target_pairs={{0,4},{1,5},{2,6},{3,7},{4,0},{5,1},{6,2},{7,3},{8,12},{9,13},{10,... | collective-permute-start | bytes 786440 | tf_op jit(solution)/shard_map/ppermute | solution.py:45
  198.7 11.3 %collective-permute-start.24 = (bf16[64,2048]{1,0:T(8,128)(2,1)S(1)}, bf16[64,2048]{1,0:T(8,128)(2,1)}, u32[]{:S(2)}, u32[]{:S(2)}) collective-permute-start(bf16[64,2048]{1,0:T(8,128)(2,1)S(1)} %get-tuple-element.83), channel_id=1, source_target_pairs={{0,6},{1,7},{2,0},{3,1},{4,2},{5,3},{6,4},{7,5},{8,14},{9,15},{10,... | collective-permute-start | bytes 786440 | tf_op jit(solution)/shard_map/ppermute | solution.py:45
  (14 other events, 288.6 us)
Sparse Core Ops, SparseCore 0:
  10.7 58.8 all-gather.3
  71.8 71.3 all-gather.5
